TPU v7x, 512 devices: a whole 4x8x8 slice. The times are simulated.
512 devices in a mesh: depth: 8 (over y), row: 8 (over x, core), col: 8 (over z).
Axes of the slice: x: 4, y: 8, z: 8, core: 2. Of those that a mesh axis runs over, the one named last changes fastest.
Arguments:
- state: float32 [4, 128, 128, 1024], P(None, 'depth', 'row', 'col'), may hold values from 0 to 1
- velocity: float32 [3, 128, 128, 1024], P(None, 'depth', 'row', 'col'), may hold values from -3 to 3
- view_order: int32 [8, 8], P('row', 'col'), may hold values from 0 to 1
- tf_table: int32 [4, 256], replicated, may hold values from 0 to 255
Outputs:
- new_state: float32 [4, 128, 128, 1024], P(None, 'depth', 'row', 'col')
- image: float32 [4, 512, 512], P(None, 'row', 'col')
Inputs may be any that keep to these rules, and one draw needn't show every extreme that they name: `view_order`: 0 puts the lowest depth indices in front, 1 the highest. `tf_table`: levels in units of 1/255.
All inputs are finite; a program needn't handle non-finite values.
Results may differ from a plain program's by a relative error of at most 0.0003.
Values sent between devices are 32-bit elements; how exact they have to be, the bound alone decides.
A program may use at most 128 MiB of HBM per device.

v0:
```python
import jax
import jax.numpy as jnp
import numpy as np
from jax import lax
from jax.sharding import PartitionSpec as P

PIX_R = 64
PIX_C = 64


FIRST_COEF = (0.8, -0.2, 4.0 / 105.0, -1.0 / 280.0)
SECOND_COEF = (1.6, -0.2, 8.0 / 315.0, -1.0 / 560.0)
CENTER_COEF = -205.0 / 72.0
DIFFUSIVITY = (0.05, 0.04, 0.03, 0.08)
TIME_STEP = 0.2
RATE_CONST = 2.0
IGNITION_SLOPE = 8.0
IGNITION_TEMP = 0.5
OXIDIZER_RATIO = 1.5
HEAT_RELEASE = 0.8
SHEAR_CELLS = 2.0
OPACITY_TOTAL = 6.0


def extended(shard, sides, width):
    edges = {}
    for axis, dim in sides:
        devices, length = (lax.axis_size(axis), shard.shape[dim])
        up = [(i, (i + 1) % devices) for i in range(devices)]
        last = lax.slice_in_dim(shard, length - width, length, axis=dim)
        initial = lax.slice_in_dim(shard, 0, width, axis=dim)
        edges[dim] = (
            lax.ppermute(last, axis, up),
            lax.ppermute(initial, axis, [(b, a) for a, b in up]),
        )
    done = []
    for _, dim in sides:
        low, high = edges[dim]
        around = [(width, width) if d in done else (0, 0) for d in range(shard.ndim)]
        shard = jnp.concatenate([jnp.pad(low, around), shard, jnp.pad(high, around)], axis=dim)
        done.append(dim)
    return shard


def partner(value, axis, distance):
    mask = 2**distance
    pairs = [(source, source ^ mask) for source in range(lax.axis_size(axis))]
    return lax.ppermute(value, axis, pairs)


def copy_for_each(shard, axis):
    copies = jnp.broadcast_to(shard, (lax.axis_size(axis), *shard.shape))
    return lax.all_to_all(copies, axis, split_axis=0, concat_axis=0, tiled=True)


def joined_along(pieces, dim):
    lengths = list(pieces.shape[1:])
    lengths[dim] *= pieces.shape[0]
    return jnp.moveaxis(pieces, 0, dim).reshape(lengths)


def gather_directly(shard, axis, dim):
    pieces = copy_for_each(shard, axis)
    return joined_along(pieces, dim)


def source_terms(centre):
    rate = (
        RATE_CONST
        * centre[0]
        * centre[1]
        * jax.nn.sigmoid(IGNITION_SLOPE * (centre[3] - IGNITION_TEMP))
    )
    return jnp.stack(
        [-rate, -OXIDIZER_RATIO * rate, (1.0 + OXIDIZER_RATIO) * rate, HEAT_RELEASE * rate]
    )


def combine_terms(centre, gradients, laplace, velocity):
    advect = (
        velocity[0][None] * gradients[0]
        + velocity[1][None] * gradients[1]
        + velocity[2][None] * gradients[2]
    )
    diffusion = jnp.stack(
        [DIFFUSIVITY[field_index] * laplace[field_index] for field_index in range(4)]
    )
    return diffusion - advect + source_terms(centre)


def tendency(padded, velocity):
    depth_cells = padded.shape[1] - 8
    row_cells = padded.shape[2] - 8
    column_cells = padded.shape[3] - 8

    def window(shifts):
        begin = (0, 4 + shifts[0], 4 + shifts[1], 4 + shifts[2])
        finish = (
            padded.shape[0],
            begin[1] + depth_cells,
            begin[2] + row_cells,
            begin[3] + column_cells,
        )
        return lax.slice(padded, begin, finish)

    centre = window((0, 0, 0))
    laplace = 3.0 * CENTER_COEF * centre
    gradients = []
    for spatial in range(3):
        gradient = jnp.zeros_like(centre)
        for offset in range(4):
            ahead_shift = tuple(
                (offset + 1 if dimension == spatial else 0 for dimension in range(3))
            )
            behind_shift = tuple(
                (-(offset + 1) if dimension == spatial else 0 for dimension in range(3))
            )
            forward = window(ahead_shift)
            backward = window(behind_shift)
            gradient = gradient + FIRST_COEF[offset] * (forward - backward)
            laplace = laplace + SECOND_COEF[offset] * (forward + backward)
        gradients.append(gradient)
    return combine_terms(centre, gradients, laplace, velocity)


def section_padding(fields):
    return extended(fields, (("depth", 1), ("row", 2), ("col", 3)), 4)


def row_matrix(first_slice, slice_count, slice_total, cell_count, pixels):
    stride = cell_count / pixels
    spread = max(1.0, stride)
    centres = (jnp.arange(pixels, dtype=jnp.float32) + 0.5) * stride - 0.5
    global_slices = (first_slice + jnp.arange(slice_count, dtype=jnp.int32)).astype(jnp.float32)
    shifts = SHEAR_CELLS * ((global_slices + 0.5) / slice_total - 0.5)
    places = jnp.clip(centres[None, :] + shifts[:, None], 0.0, cell_count - 1.0)
    cells_at = jnp.arange(cell_count, dtype=jnp.float32)
    return (
        jnp.maximum(0.0, 1.0 - jnp.abs(places[:, :, None] - cells_at[None, None, :]) / spread)
        / spread
    )


def column_matrix(cell_count, pixels):
    stride = cell_count / pixels
    spread = max(1.0, stride)
    centres = jnp.clip(
        (jnp.arange(pixels, dtype=jnp.float32) + 0.5) * stride - 0.5, 0.0, cell_count - 1.0
    )
    cells_at = jnp.arange(cell_count, dtype=jnp.float32)
    return jnp.maximum(0.0, 1.0 - jnp.abs(centres[None, :] - cells_at[:, None]) / spread) / spread


def shade(values, table_values, slice_total):
    levels = table_values.shape[1]
    level = jnp.clip(values, 0.0, 1.0) * (levels - 1.0)
    marks = jnp.arange(levels, dtype=jnp.float32)
    weights = jnp.maximum(0.0, 1.0 - jnp.abs(level[None, :] - marks[:, None]))
    raw_colour = jnp.dot(
        table_values, weights, preferred_element_type=jnp.float32, precision=lax.Precision.HIGHEST
    ) * (1.0 / 255.0)
    opacity = OPACITY_TOTAL / slice_total * raw_colour[3]
    return jnp.concatenate([opacity[None, :] * raw_colour[:3], opacity[None, :]], 0)


def march_slices(sampled, table_values, order_flag, slice_total):
    slice_count = sampled.shape[0]

    def advance(running, position):
        accumulated, transmit = running
        chosen = jnp.where(order_flag == 0, position, slice_count - 1 - position)
        values = lax.dynamic_index_in_dim(sampled, chosen, 0, keepdims=False)
        colour = shade(values, table_values, slice_total)
        return ((accumulated + transmit[None, :] * colour, transmit * (1.0 - colour[3])), None)

    start = (
        jnp.zeros((4, sampled.shape[1]), jnp.float32),
        jnp.ones((sampled.shape[1],), jnp.float32),
    )
    finished, unused = lax.scan(advance, start, jnp.arange(slice_count, dtype=jnp.int32))
    return finished[0]


def composite_over(front_part, back_part):
    return front_part + (1.0 - front_part[3:4]) * back_part


def reversed_bits(count, bit_total):
    result = []
    for position in range(count):
        flipped = 0
        for bit_number in range(bit_total):
            if position >> bit_number & 1:
                flipped = flipped | 1 << bit_total - 1 - bit_number
        result.append(flipped)
    return np.array(result, dtype=np.int32)


def local(state, velocity, view_order, tf_table):
    first_rate = tendency(section_padding(state), velocity)
    middle = state + TIME_STEP * first_rate
    second_rate = tendency(section_padding(middle), velocity)
    new_state = state + 0.5 * TIME_STEP * (first_rate + second_rate)
    slice_count = state.shape[1]
    depth_index = lax.axis_index("depth")
    depth_count = lax.axis_size("depth")
    bit_total = depth_count.bit_length() - 1
    slice_total = slice_count * depth_count
    order_flag = view_order[0, 0]
    row_weights = row_matrix(
        depth_index * slice_count, slice_count, slice_total, state.shape[2], PIX_R
    )
    column_weights = column_matrix(state.shape[3], PIX_C)
    partial_rows = jnp.einsum(
        "dpr,drc->dpc", row_weights, new_state[3], precision=lax.Precision.HIGHEST
    )
    sampled = jnp.einsum(
        "dpc,cq->dpq", partial_rows, column_weights, precision=lax.Precision.HIGHEST
    )
    sampled = sampled.reshape(slice_count, PIX_R * PIX_C)
    table_values = tf_table.astype(jnp.float32)
    brick_tile = march_slices(sampled, table_values, order_flag, slice_total)
    piece_order = np.arange(depth_count, dtype=np.int32)
    portion = brick_tile
    for bit_number in range(bit_total):
        half_width = portion.shape[1] // 2
        lower_half = portion[:, :half_width]
        upper_half = portion[:, half_width:]
        own_bit = depth_index // 2**bit_number % 2
        kept_half = jnp.where(own_bit == 0, lower_half, upper_half)
        sent_half = jnp.where(own_bit == 0, upper_half, lower_half)
        received = partner(sent_half, "depth", bit_number)
        in_front = own_bit == order_flag
        portion = jnp.where(
            in_front, composite_over(kept_half, received), composite_over(received, kept_half)
        )
    piece_order = reversed_bits(depth_count, bit_total)
    whole_tile = gather_directly(portion, "depth", 1)
    piece_width = portion.shape[1]
    pieces = whole_tile.reshape(4, depth_count, piece_width)
    placed = pieces[:, np.argsort(piece_order), :]
    return (new_state, placed.reshape(4, PIX_R, PIX_C))


def solution(mesh):
    in_specs = (
        P(None, "depth", "row", "col"),
        P(None, "depth", "row", "col"),
        P("row", "col"),
        P(),
    )
    out_specs = (P(None, "depth", "row", "col"), P(None, "row", "col"))
    return jax.shard_map(local, mesh=mesh, in_specs=in_specs, out_specs=out_specs, check_vma=False)
```

profile of v0, /device:TPU:6, one launch (start us, length us, event | category | flops | bytes accessed | tf_op | source)
XLA Modules:
  0.0 197.9 jit_solution(11375118086107122431)
XLA Ops:
  0.7 1.8 fusion.72
  2.4 3.5 %collective-permute-start.1 = (f32[4,4,16,128]{3,2,1,0:T(8,128)}, f32[4,4,16,128]{3,2,1,0:T(8,128)}, u32[]{:S(2)}, u32[]{:S(2)}) collective-permute-start(f32[4,4,16,128]{3,2,1,0:T(8,128)} %get-tuple-element.162), channel_id=1, source_target_pairs={{0,64},{64,128},{128,192},{192,256},{256,320},{320,384},{384,448},... | collective-permute-start | bytes 393224 | tf_op jit(solution)/shard_map/ppermute | solution.py:33
  5.9 3.8 %collective-permute-start = (f32[4,4,16,128]{3,2,1,0:T(8,128)}, f32[4,4,16,128]{3,2,1,0:T(8,128)S(1)}, u32[]{:S(2)}, u32[]{:S(2)}) collective-permute-start(f32[4,4,16,128]{3,2,1,0:T(8,128)} %get-tuple-element.161), channel_id=1, source_target_pairs={{64,0},{128,64},{192,128},{256,192},{320,256},{384,320},{448,384},... | collective-permute-start | bytes 393224 | tf_op jit(solution)/shard_map/ppermute | solution.py:34
  9.7 1.8 fusion.71
  12.0 1.5 fusion.70
  13.6 10.9 %collective-permute-start.4 = (f32[4,16,16,4]{3,2,1,0:T(8,128)S(1)}, f32[4,16,16,4]{3,2,1,0:T(8,128)S(1)}, u32[]{:S(2)}, u32[]{:S(2)}) collective-permute-start(f32[4,16,16,4]{3,2,1,0:T(8,128)S(1)} %get-tuple-element.157), channel_id=1, source_target_pairs={{1,0},{2,1},{3,2},{4,3},{5,4},{6,5},{7,6},{0,7},{9,8},{10,9},{11,1... | collective-permute-start | bytes 49160 | tf_op jit(solution)/shard_map/ppermute | solution.py:34
  25.5 1.9 collective-permute-start.5
  27.5 0.9 constant_dynamic-update-slice_fusion.3
  28.7 7.1 %collective-permute-done.4 = f32[4,16,16,4]{3,2,1,0:T(8,128)S(1)} collective-permute-done((f32[4,16,16,4]{3,2,1,0:T(8,128)S(1)}, f32[4,16,16,4]{3,2,1,0:T(8,128)S(1)}, u32[]{:S(2)}, u32[]{:S(2)}) %collective-permute-start.4) | collective-permute-done | bytes 16416 | tf_op jit(solution)/shard_map/ppermute | solution.py:34
  35.8 6.9 %collective-permute-done.5 = f32[4,16,16,4]{3,2,1,0:T(8,128)S(1)} collective-permute-done((f32[4,16,16,4]{3,2,1,0:T(8,128)S(1)}, f32[4,16,16,4]{3,2,1,0:T(8,128)S(1)}, u32[]{:S(2)}, u32[]{:S(2)}) %collective-permute-start.5) | collective-permute-done | bytes 16416 | tf_op jit(solution)/shard_map/ppermute | solution.py:33
  42.7 1.3 select_maximum_fusion.3
  44.0 1.5 multiply_add_fusion.2
  45.6 1.9 multiply_add_fusion.1
  48.4 4.1 %collective-permute-start.6 = (f32[4,4,16,128]{3,2,1,0:T(8,128)S(1)}, f32[4,4,16,128]{3,2,1,0:T(8,128)S(1)}, u32[]{:S(2)}, u32[]{:S(2)}) collective-permute-start(f32[4,4,16,128]{3,2,1,0:T(8,128)S(1)} %get-tuple-element.149), channel_id=1, source_target_pairs={{64,0},{128,64},{192,128},{256,192},{320,256},{384,320},{448,384},... | collective-permute-start | bytes 393224 | tf_op jit(solution)/shard_map/ppermute | solution.py:34
  52.6 1.9 collective-permute-start.7
  54.5 1.9 collective-permute-start.10
  56.5 4.1 %collective-permute-start.11 = (f32[4,16,16,4]{3,2,1,0:T(8,128)S(1)}, f32[4,16,16,4]{3,2,1,0:T(8,128)S(1)}, u32[]{:S(2)}, u32[]{:S(2)}) collective-permute-start(f32[4,16,16,4]{3,2,1,0:T(8,128)S(1)} %get-tuple-element.145), channel_id=1, source_target_pairs={{0,1},{1,2},{2,3},{3,4},{4,5},{5,6},{6,7},{7,0},{8,9},{9,10},{10,1... | collective-permute-start | bytes 49160 | tf_op jit(solution)/shard_map/ppermute | solution.py:33
  60.9 8.8 %collective-permute-done.10 = f32[4,16,16,4]{3,2,1,0:T(8,128)S(1)} collective-permute-done((f32[4,16,16,4]{3,2,1,0:T(8,128)S(1)}, f32[4,16,16,4]{3,2,1,0:T(8,128)S(1)}, u32[]{:S(2)}, u32[]{:S(2)}) %collective-permute-start.10) | collective-permute-done | bytes 16416 | tf_op jit(solution)/shard_map/ppermute | solution.py:34
  69.7 3.2 %collective-permute-done.11 = f32[4,16,16,4]{3,2,1,0:T(8,128)S(1)} collective-permute-done((f32[4,16,16,4]{3,2,1,0:T(8,128)S(1)}, f32[4,16,16,4]{3,2,1,0:T(8,128)S(1)}, u32[]{:S(2)}, u32[]{:S(2)}) %collective-permute-start.11) | collective-permute-done | bytes 16416 | tf_op jit(solution)/shard_map/ppermute | solution.py:33
  72.9 1.8 select_maximum_fusion.1
  74.7 1.3 multiply_add_fusion
  76.1 2.0 %fusion.28 = f32[4,16,16,128]{3,2,1,0:T(8,128)S(1)} fusion(f32[4,16,16,128]{3,2,1,0:T(8,128)S(1)} %copy-done, f32[4,16,16,128]{3,2,1,0:T(8,128)S(1)} %get-tuple-element.129, f32[1,16,16,128]{3,2,1,0:T(8,128)S(1)} %get-tuple-element.141, f32[1,16,16,128]{3,2,1,0:T(8,128)S(1)} %get-tuple-element.142, f32[1,16,16,128]{3,2,1,0:T(8,128)S(1)} %get-tuple-element.143, ...), kind=kLoop, calls=%fused_computation.74 | loop fusion | flops 7471104 | bytes 12189696 | tf_op jit(solution)/shard_map/add | solution.py:203
  78.1 1.0 fusion.29
  80.0 78.2 %while.15 = (s32[]{:T(128)}, f32[4,4096]{1,0:T(4,128)S(1)}, f32[4096]{0:T(1024)S(1)}, s32[16]{0:T(128)S(1)}, pred[]{:T(512)}, /*index=5*/f32[16,4096]{1,0:T(8,12...) while((s32[]{:T(128)}, f32[4,4096]{1,0:T(4,128)S(1)}, ...), condition=%wide.region_1.2_spmd.clone, body=%wide.region_0.1_spmd.clone.sunk | while | flops 54644744 | bytes 561347 | solution.py:180
  81.9 2.8 %fusion.82 = f32[4,4096]{1,0:T(4,128)S(1)} fusion(f32[4,256]{1,0:T(4,128)S(1)} %get-tuple-element.261, f32[4096]{0:T(1024)S(1)} %bitcast.47), kind=kOutput, calls=%fused_computation.2.clone.1 | convolution fusion | flops 54542336 | bytes 86016 | tf_op jit(solution)/shard_map/while/body/eval_jaxpr/dot_general | solution.py:159
  86.8 2.8 %fusion.82 = f32[4,4096]{1,0:T(4,128)S(1)} fusion(f32[4,256]{1,0:T(4,128)S(1)} %get-tuple-element.261, f32[4096]{0:T(1024)S(1)} %bitcast.47), kind=kOutput, calls=%fused_computation.2.clone.1 | convolution fusion | flops 54542336 | bytes 86016 | tf_op jit(solution)/shard_map/while/body/eval_jaxpr/dot_general | solution.py:159
  91.7 2.8 %fusion.82 = f32[4,4096]{1,0:T(4,128)S(1)} fusion(f32[4,256]{1,0:T(4,128)S(1)} %get-tuple-element.261, f32[4096]{0:T(1024)S(1)} %bitcast.47), kind=kOutput, calls=%fused_computation.2.clone.1 | convolution fusion | flops 54542336 | bytes 86016 | tf_op jit(solution)/shard_map/while/body/eval_jaxpr/dot_general | solution.py:159
  96.6 2.8 %fusion.82 = f32[4,4096]{1,0:T(4,128)S(1)} fusion(f32[4,256]{1,0:T(4,128)S(1)} %get-tuple-element.261, f32[4096]{0:T(1024)S(1)} %bitcast.47), kind=kOutput, calls=%fused_computation.2.clone.1 | convolution fusion | flops 54542336 | bytes 86016 | tf_op jit(solution)/shard_map/while/body/eval_jaxpr/dot_general | solution.py:159
  101.5 2.8 %fusion.82 = f32[4,4096]{1,0:T(4,128)S(1)} fusion(f32[4,256]{1,0:T(4,128)S(1)} %get-tuple-element.261, f32[4096]{0:T(1024)S(1)} %bitcast.47), kind=kOutput, calls=%fused_computation.2.clone.1 | convolution fusion | flops 54542336 | bytes 86016 | tf_op jit(solution)/shard_map/while/body/eval_jaxpr/dot_general | solution.py:159
  106.4 2.8 %fusion.82 = f32[4,4096]{1,0:T(4,128)S(1)} fusion(f32[4,256]{1,0:T(4,128)S(1)} %get-tuple-element.261, f32[4096]{0:T(1024)S(1)} %bitcast.47), kind=kOutput, calls=%fused_computation.2.clone.1 | convolution fusion | flops 54542336 | bytes 86016 | tf_op jit(solution)/shard_map/while/body/eval_jaxpr/dot_general | solution.py:159
  111.2 2.8 %fusion.82 = f32[4,4096]{1,0:T(4,128)S(1)} fusion(f32[4,256]{1,0:T(4,128)S(1)} %get-tuple-element.261, f32[4096]{0:T(1024)S(1)} %bitcast.47), kind=kOutput, calls=%fused_computation.2.clone.1 | convolution fusion | flops 54542336 | bytes 86016 | tf_op jit(solution)/shard_map/while/body/eval_jaxpr/dot_general | solution.py:159
  116.1 2.8 %fusion.82 = f32[4,4096]{1,0:T(4,128)S(1)} fusion(f32[4,256]{1,0:T(4,128)S(1)} %get-tuple-element.261, f32[4096]{0:T(1024)S(1)} %bitcast.47), kind=kOutput, calls=%fused_computation.2.clone.1 | convolution fusion | flops 54542336 | bytes 86016 | tf_op jit(solution)/shard_map/while/body/eval_jaxpr/dot_general | solution.py:159
  121.0 2.8 %fusion.82 = f32[4,4096]{1,0:T(4,128)S(1)} fusion(f32[4,256]{1,0:T(4,128)S(1)} %get-tuple-element.261, f32[4096]{0:T(1024)S(1)} %bitcast.47), kind=kOutput, calls=%fused_computation.2.clone.1 | convolution fusion | flops 54542336 | bytes 86016 | tf_op jit(solution)/shard_map/while/body/eval_jaxpr/dot_general | solution.py:159
  125.9 2.8 %fusion.82 = f32[4,4096]{1,0:T(4,128)S(1)} fusion(f32[4,256]{1,0:T(4,128)S(1)} %get-tuple-element.261, f32[4096]{0:T(1024)S(1)} %bitcast.47), kind=kOutput, calls=%fused_computation.2.clone.1 | convolution fusion | flops 54542336 | bytes 86016 | tf_op jit(solution)/shard_map/while/body/eval_jaxpr/dot_general | solution.py:159
  130.8 2.8 %fusion.82 = f32[4,4096]{1,0:T(4,128)S(1)} fusion(f32[4,256]{1,0:T(4,128)S(1)} %get-tuple-element.261, f32[4096]{0:T(1024)S(1)} %bitcast.47), kind=kOutput, calls=%fused_computation.2.clone.1 | convolution fusion | flops 54542336 | bytes 86016 | tf_op jit(solution)/shard_map/while/body/eval_jaxpr/dot_general | solution.py:159
  135.7 2.8 %fusion.82 = f32[4,4096]{1,0:T(4,128)S(1)} fusion(f32[4,256]{1,0:T(4,128)S(1)} %get-tuple-element.261, f32[4096]{0:T(1024)S(1)} %bitcast.47), kind=kOutput, calls=%fused_computation.2.clone.1 | convolution fusion | flops 54542336 | bytes 86016 | tf_op jit(solution)/shard_map/while/body/eval_jaxpr/dot_general | solution.py:159
  140.6 2.8 %fusion.82 = f32[4,4096]{1,0:T(4,128)S(1)} fusion(f32[4,256]{1,0:T(4,128)S(1)} %get-tuple-element.261, f32[4096]{0:T(1024)S(1)} %bitcast.47), kind=kOutput, calls=%fused_computation.2.clone.1 | convolution fusion | flops 54542336 | bytes 86016 | tf_op jit(solution)/shard_map/while/body/eval_jaxpr/dot_general | solution.py:159
  145.5 2.8 %fusion.82 = f32[4,4096]{1,0:T(4,128)S(1)} fusion(f32[4,256]{1,0:T(4,128)S(1)} %get-tuple-element.261, f32[4096]{0:T(1024)S(1)} %bitcast.47), kind=kOutput, calls=%fused_computation.2.clone.1 | convolution fusion | flops 54542336 | bytes 86016 | tf_op jit(solution)/shard_map/while/body/eval_jaxpr/dot_general | solution.py:159
  150.4 2.8 %fusion.82 = f32[4,4096]{1,0:T(4,128)S(1)} fusion(f32[4,256]{1,0:T(4,128)S(1)} %get-tuple-element.261, f32[4096]{0:T(1024)S(1)} %bitcast.47), kind=kOutput, calls=%fused_computation.2.clone.1 | convolution fusion | flops 54542336 | bytes 86016 | tf_op jit(solution)/shard_map/while/body/eval_jaxpr/dot_general | solution.py:159
  155.2 2.8 %fusion.82 = f32[4,4096]{1,0:T(4,128)S(1)} fusion(f32[4,256]{1,0:T(4,128)S(1)} %get-tuple-element.261, f32[4096]{0:T(1024)S(1)} %bitcast.47), kind=kOutput, calls=%fused_computation.2.clone.1 | convolution fusion | flops 54542336 | bytes 86016 | tf_op jit(solution)/shard_map/while/body/eval_jaxpr/dot_general | solution.py:159
  158.2 2.1 %collective-permute-start.12 = (f32[4,2048]{1,0:T(4,128)S(1)}, f32[4,2048]{1,0:T(4,128)S(1)}, u32[]{:S(2)}, u32[]{:S(2)}) collective-permute-start(f32[4,2048]{1,0:T(4,128)S(1)} %get-tuple-element.177), channel_id=1, source_target_pairs={{0,64},{64,0},{128,192},{192,128},{256,320},{320,256},{384,448},{4... | collective-permute-start | bytes 98312 | tf_op jit(solution)/shard_map/ppermute | solution.py:48
  160.4 3.7 %collective-permute-done.12 = f32[4,2048]{1,0:T(4,128)S(1)} collective-permute-done((f32[4,2048]{1,0:T(4,128)S(1)}, f32[4,2048]{1,0:T(4,128)S(1)}, u32[]{:S(2)}, u32[]{:S(2)}) %collective-permute-start.12) | collective-permute-done | bytes 32800 | tf_op jit(solution)/shard_map/ppermute | solution.py:48
  164.1 4.6 %collective-permute-start.13 = (f32[4,1024]{1,0:T(4,128)S(1)}, f32[4,1024]{1,0:T(4,128)S(1)}, u32[]{:S(2)}, u32[]{:S(2)}) collective-permute-start(f32[4,1024]{1,0:T(4,128)S(1)} %get-tuple-element.179), channel_id=1, source_target_pairs={{0,128},{64,192},{128,0},{192,64},{256,384},{320,448},{384,256},{4... | collective-permute-start | bytes 49160 | tf_op jit(solution)/shard_map/ppermute | solution.py:48
  168.7 1.9 collective-permute-done.13
  170.7 8.0 %collective-permute-start.14 = (f32[4,512]{1,0:T(4,128)S(1)}, f32[4,512]{1,0:T(4,128)S(1)}, u32[]{:S(2)}, u32[]{:S(2)}) collective-permute-start(f32[4,512]{1,0:T(4,128)S(1)} %get-tuple-element.181), channel_id=1, source_target_pairs={{0,256},{64,320},{128,384},{192,448},{256,0},{320,64},{384,128},{4... | collective-permute-start | bytes 24584 | tf_op jit(solution)/shard_map/ppermute | solution.py:48
  178.7 1.6 collective-permute-done.14
  181.0 7.2 %all-to-all-start = ((f32[8,4,512]{2,1,0:T(4,128)}), f32[8,4,512]{2,1,0:T(4,128)S(1)}, u32[]{:S(2)}, u32[]{:S(2)}) async-start(f32[8,4,512]{2,1,0:T(4,128)} %broadcast_in_dim.7), calls=%async_computation | async-start | bytes 131072 | tf_op jit(solution)/shard_map/all_to_all | solution.py:53
  188.2 8.4 %all-to-all-done = f32[8,4,512]{2,1,0:T(4,128)S(1)} async-done(((f32[8,4,512]{2,1,0:T(4,128)}), f32[8,4,512]{2,1,0:T(4,128)S(1)}, u32[]{:S(2)}, u32[]{:S(2)}) %all-to-all-start) | async-done | bytes 65568 | tf_op jit(solution)/shard_map/all_to_all | solution.py:53
  (162 shorter events, 17.3 us)
Async XLA Ops:
  0.6 23.9 %copy-start = (f32[4,16,16,128]{3,2,1,0:T(8,128)S(1)}, f32[4,16,16,128]{3,2,1,0:T(8,128)}, u32[]{:S(2)}) copy-start(f32[4,16,16,128]{3,2,1,0:T(8,128)} %param.8) | copy-start | bytes 1572868
  0.6 24.0 %copy-start.2 = (f32[3,16,16,128]{3,2,1,0:T(8,128)S(1)}, f32[3,16,16,128]{3,2,1,0:T(8,128)}, u32[]{:S(2)}) copy-start(f32[3,16,16,128]{3,2,1,0:T(8,128)} %param.9) | copy-start | bytes 1179652
  2.4 23.1 %collective-permute-start.1 = (f32[4,4,16,128]{3,2,1,0:T(8,128)}, f32[4,4,16,128]{3,2,1,0:T(8,128)}, u32[]{:S(2)}, u32[]{:S(2)}) collective-permute-start(f32[4,4,16,128]{3,2,1,0:T(8,128)} %get-tuple-element.162), channel_id=1, source_target_pairs={{0,64},{64,128},{128,192},{192,256},{256,320},{320,384},{384,448},... | collective-permute-start | bytes 393224 | tf_op jit(solution)/shard_map/ppermute | solution.py:33
  5.9 19.5 %copy-start.3 = (s32[4,256]{1,0:T(4,128)S(1)}, s32[4,256]{1,0:T(4,128)}, u32[]{:S(2)}) copy-start(s32[4,256]{1,0:T(4,128)} %param.11) | copy-start | bytes 12292
  5.9 22.6 %collective-permute-start = (f32[4,4,16,128]{3,2,1,0:T(8,128)}, f32[4,4,16,128]{3,2,1,0:T(8,128)S(1)}, u32[]{:S(2)}, u32[]{:S(2)}) collective-permute-start(f32[4,4,16,128]{3,2,1,0:T(8,128)} %get-tuple-element.161), channel_id=1, source_target_pairs={{64,0},{128,64},{192,128},{256,192},{320,256},{384,320},{448,384},... | collective-permute-start | bytes 393224 | tf_op jit(solution)/shard_map/ppermute | solution.py:34
  11.5 17.0 %collective-permute-start.2 = (f32[4,16,4,128]{3,2,1,0:T(4,128)}, f32[4,16,4,128]{3,2,1,0:T(4,128)S(1)}, u32[]{:S(2)}, u32[]{:S(2)}) collective-permute-start(f32[4,16,4,128]{3,2,1,0:T(4,128)} %get-tuple-element.160), channel_id=1, source_target_pairs={{8,0},{16,8},{24,16},{32,24},{40,32},{48,40},{56,48},{0,56},{9,1},... | collective-permute-start | bytes 393224 | tf_op jit(solution)/shard_map/ppermute | solution.py:34
  11.5 17.1 %collective-permute-start.3 = (f32[4,16,4,128]{3,2,1,0:T(4,128)}, f32[4,16,4,128]{3,2,1,0:T(4,128)S(1)}, u32[]{:S(2)}, u32[]{:S(2)}) collective-permute-start(f32[4,16,4,128]{3,2,1,0:T(4,128)} %get-tuple-element.159), channel_id=1, source_target_pairs={{0,8},{8,16},{16,24},{24,32},{32,40},{40,48},{48,56},{56,0},{1,9},... | collective-permute-start | bytes 393224 | tf_op jit(solution)/shard_map/ppermute | solution.py:33
  13.6 22.2 %collective-permute-start.4 = (f32[4,16,16,4]{3,2,1,0:T(8,128)S(1)}, f32[4,16,16,4]{3,2,1,0:T(8,128)S(1)}, u32[]{:S(2)}, u32[]{:S(2)}) collective-permute-start(f32[4,16,16,4]{3,2,1,0:T(8,128)S(1)} %get-tuple-element.157), channel_id=1, source_target_pairs={{1,0},{2,1},{3,2},{4,3},{5,4},{6,5},{7,6},{0,7},{9,8},{10,9},{11,1... | collective-permute-start | bytes 49160 | tf_op jit(solution)/shard_map/ppermute | solution.py:34
  25.5 17.2 %collective-permute-start.5 = (f32[4,16,16,4]{3,2,1,0:T(8,128)S(1)}, f32[4,16,16,4]{3,2,1,0:T(8,128)S(1)}, u32[]{:S(2)}, u32[]{:S(2)}) collective-permute-start(f32[4,16,16,4]{3,2,1,0:T(8,128)S(1)} %get-tuple-element.158), channel_id=1, source_target_pairs={{0,1},{1,2},{2,3},{3,4},{4,5},{5,6},{6,7},{7,0},{8,9},{9,10},{10,1... | collective-permute-start | bytes 49160 | tf_op jit(solution)/shard_map/ppermute | solution.py:33
  47.8 8.6 %collective-permute-start.8 = (f32[4,16,4,128]{3,2,1,0:T(4,128)S(1)}, f32[4,16,4,128]{3,2,1,0:T(4,128)S(1)}, u32[]{:S(2)}, u32[]{:S(2)}) collective-permute-start(f32[4,16,4,128]{3,2,1,0:T(4,128)S(1)} %get-tuple-element.147), channel_id=1, source_target_pairs={{8,0},{16,8},{24,16},{32,24},{40,32},{48,40},{56,48},{0,56},{9,1},... | collective-permute-start | bytes 393224 | tf_op jit(solution)/shard_map/ppermute | solution.py:34
  48.3 12.4 %collective-permute-start.9 = (f32[4,16,4,128]{3,2,1,0:T(4,128)S(1)}, f32[4,16,4,128]{3,2,1,0:T(4,128)S(1)}, u32[]{:S(2)}, u32[]{:S(2)}) collective-permute-start(f32[4,16,4,128]{3,2,1,0:T(4,128)S(1)} %get-tuple-element.146), channel_id=1, source_target_pairs={{0,8},{8,16},{16,24},{24,32},{32,40},{40,48},{48,56},{56,0},{1,9},... | collective-permute-start | bytes 393224 | tf_op jit(solution)/shard_map/ppermute | solution.py:33
  48.4 12.2 %collective-permute-start.6 = (f32[4,4,16,128]{3,2,1,0:T(8,128)S(1)}, f32[4,4,16,128]{3,2,1,0:T(8,128)S(1)}, u32[]{:S(2)}, u32[]{:S(2)}) collective-permute-start(f32[4,4,16,128]{3,2,1,0:T(8,128)S(1)} %get-tuple-element.149), channel_id=1, source_target_pairs={{64,0},{128,64},{192,128},{256,192},{320,256},{384,320},{448,384},... | collective-permute-start | bytes 393224 | tf_op jit(solution)/shard_map/ppermute | solution.py:34
  52.6 8.1 %collective-permute-start.7 = (f32[4,4,16,128]{3,2,1,0:T(8,128)S(1)}, f32[4,4,16,128]{3,2,1,0:T(8,128)S(1)}, u32[]{:S(2)}, u32[]{:S(2)}) collective-permute-start(f32[4,4,16,128]{3,2,1,0:T(8,128)S(1)} %get-tuple-element.148), channel_id=1, source_target_pairs={{0,64},{64,128},{128,192},{192,256},{256,320},{320,384},{384,448},... | collective-permute-start | bytes 393224 | tf_op jit(solution)/shard_map/ppermute | solution.py:33
  54.5 15.2 %collective-permute-start.10 = (f32[4,16,16,4]{3,2,1,0:T(8,128)S(1)}, f32[4,16,16,4]{3,2,1,0:T(8,128)S(1)}, u32[]{:S(2)}, u32[]{:S(2)}) collective-permute-start(f32[4,16,16,4]{3,2,1,0:T(8,128)S(1)} %get-tuple-element.144), channel_id=1, source_target_pairs={{1,0},{2,1},{3,2},{4,3},{5,4},{6,5},{7,6},{0,7},{9,8},{10,9},{11,1... | collective-permute-start | bytes 49160 | tf_op jit(solution)/shard_map/ppermute | solution.py:34
  56.5 16.4 %collective-permute-start.11 = (f32[4,16,16,4]{3,2,1,0:T(8,128)S(1)}, f32[4,16,16,4]{3,2,1,0:T(8,128)S(1)}, u32[]{:S(2)}, u32[]{:S(2)}) collective-permute-start(f32[4,16,16,4]{3,2,1,0:T(8,128)S(1)} %get-tuple-element.145), channel_id=1, source_target_pairs={{0,1},{1,2},{2,3},{3,4},{4,5},{5,6},{6,7},{7,0},{8,9},{9,10},{10,1... | collective-permute-start | bytes 49160 | tf_op jit(solution)/shard_map/ppermute | solution.py:33
  78.1 1.9 copy-start.1
  80.0 108.2 %copy-start.4 = (s32[8]{0:T(128)S(1)}, s32[8]{0:T(128)}, u32[]{:S(2)}) copy-start(s32[8]{0:T(128)} %constant.209) | copy-start | bytes 100
  158.2 5.8 %collective-permute-start.12 = (f32[4,2048]{1,0:T(4,128)S(1)}, f32[4,2048]{1,0:T(4,128)S(1)}, u32[]{:S(2)}, u32[]{:S(2)}) collective-permute-start(f32[4,2048]{1,0:T(4,128)S(1)} %get-tuple-element.177), channel_id=1, source_target_pairs={{0,64},{64,0},{128,192},{192,128},{256,320},{320,256},{384,448},{4... | collective-permute-start | bytes 98312 | tf_op jit(solution)/shard_map/ppermute | solution.py:48
  164.1 6.5 %collective-permute-start.13 = (f32[4,1024]{1,0:T(4,128)S(1)}, f32[4,1024]{1,0:T(4,128)S(1)}, u32[]{:S(2)}, u32[]{:S(2)}) collective-permute-start(f32[4,1024]{1,0:T(4,128)S(1)} %get-tuple-element.179), channel_id=1, source_target_pairs={{0,128},{64,192},{128,0},{192,64},{256,384},{320,448},{384,256},{4... | collective-permute-start | bytes 49160 | tf_op jit(solution)/shard_map/ppermute | solution.py:48
  170.7 9.7 %collective-permute-start.14 = (f32[4,512]{1,0:T(4,128)S(1)}, f32[4,512]{1,0:T(4,128)S(1)}, u32[]{:S(2)}, u32[]{:S(2)}) collective-permute-start(f32[4,512]{1,0:T(4,128)S(1)} %get-tuple-element.181), channel_id=1, source_target_pairs={{0,256},{64,320},{128,384},{192,448},{256,0},{320,64},{384,128},{4... | collective-permute-start | bytes 24584 | tf_op jit(solution)/shard_map/ppermute | solution.py:48
  181.0 15.6 %all-to-all-start = ((f32[8,4,512]{2,1,0:T(4,128)}), f32[8,4,512]{2,1,0:T(4,128)S(1)}, u32[]{:S(2)}, u32[]{:S(2)}) async-start(f32[8,4,512]{2,1,0:T(4,128)} %broadcast_in_dim.7), calls=%async_computation | async-start | bytes 131072 | tf_op jit(solution)/shard_map/all_to_all | solution.py:53
where the time goes:
time: 200 us; the launch traced here: 198 us
  starting transfers between devices  55.3 us (28%)
  matrix products  46.3 us (23%)
  waiting for transfers between devices  41.6 us (21%)
  loops' own time  21.5 us (11%)
  local copies, waits for them, and re-layouts  18.2 us (9%)
  other arithmetic  13.3 us (7%)
    dot_general x16, matrix products, shade(): jnp.dot(table_values, weights, preferred_element_type=jnp.float32, precis...  44.6 us
    another operation x1, loops' own time, march_slices(): lax.scan(advance, start, jnp.arange(slice_count, dtype=jnp.int32))  21.5 us
    ppermute x6, starting transfers between devices, extended(): lax.ppermute(initial, axis, [(b, a) for a, b in up])  21.2 us
    ppermute x6, waiting for transfers between devices, extended(): lax.ppermute(initial, axis, [(b, a) for a, b in up])  15.9 us
    ppermute x3, starting transfers between devices, partner(): return lax.ppermute(value, axis, pairs)  14.8 us
    ppermute x6, starting transfers between devices, extended(): lax.ppermute(last, axis, up)  12.1 us
    ppermute x6, waiting for transfers between devices, extended(): lax.ppermute(last, axis, up)  10.1 us
    dynamic_slice x16, local copies, waits for them, and re-layouts, march_slices(): lax.scan(advance, start, jnp.arange(slice_count, dtype=jnp.int32))  9.38 us
  transfers between devices with their start and end apart: 16, of which 8 were waited for; matrix products, arithmetic and copies ran while one was open for 3% of the time, Pallas kernels for 0%

commit v1 on v0

v1 whole, which is shorter than its diff:
```python
import functools

import jax
import jax.numpy as jnp
from jax import lax
from jax.experimental import pallas as pl
from jax.experimental.pallas import tpu as pltpu
from jax.sharding import PartitionSpec as P

MESH = pl.DeviceIdType.MESH
FIRST_COEF = (0.8, -0.2, 4.0 / 105.0, -1.0 / 280.0)
SECOND_COEF = (1.6, -0.2, 8.0 / 315.0, -1.0 / 560.0)
CENTER_COEF = -205.0 / 72.0
DIFFUSIVITY = (0.05, 0.04, 0.03, 0.08)
SOURCE = (-1.0, -1.5, 2.5, 0.8)
FIELDS = (3, 0, 1, 2)
ND = 16
NR = 16
LANES = 128
TOP = 8
GROUP = 2
SLICES = 128
PIX = 64


def kernel(sizes, state, velocity, order, table, new_state, image, ext1, ext2, vel, rate, out, pack, got, texture,
           part, mixed, final, in_sem, vel_sem, out_sem, send_sem, recv_sem, part_send, part_recv, fin_send, fin_recv):
    n_depth, n_row, n_col = sizes
    my_depth, my_row, my_col = lax.axis_index("depth"), lax.axis_index("row"), lax.axis_index("col")
    places = {"depth": (my_depth, n_depth), "row": (my_row, n_row), "col": (my_col, n_col)}

    def beside(axis, step):
        at, count = places[axis]
        return {axis: lax.rem(at + step + count, count)}

    barrier = pltpu.get_barrier_semaphore()
    peers = [beside("depth", step) for step in range(1, n_depth)]
    peers += [beside(axis, step) for axis in ("row", "col") for step in (1, -1)]
    for peer in peers:
        pl.semaphore_signal(barrier, inc=1, device_id=peer, device_id_type=MESH)

    def load_field(f):
        return pltpu.make_async_copy(state.at[f], ext1.at[f, 4 : 4 + ND, TOP : TOP + NR, :], in_sem.at[f])

    load_velocity = pltpu.make_async_copy(velocity, vel, vel_sem)
    for f in FIELDS:
        load_field(f).start()
    load_velocity.start()

    lane = lax.broadcasted_iota(jnp.int32, (NR, LANES), 1)
    lane_group = lane // 8

    def remote(stage, f, index, source, target, peer):
        return pltpu.make_async_remote_copy(
            src_ref=source, dst_ref=target, send_sem=send_sem.at[stage, f, index],
            recv_sem=recv_sem.at[stage, f, index], device_id=peer, device_id_type=MESH)

    def face_copies(stage, f):
        if stage == 0:
            source, target, d0, r0 = state, ext1, 0, 0
        else:
            source, target, d0, r0 = ext2, ext2, 4, TOP
        rows, layers = pl.ds(r0, NR), pl.ds(d0, ND)
        return [
            remote(stage, f, 0, source.at[f, pl.ds(d0 + ND - 4, 4), rows, :],
                   target.at[f, 0:4, TOP : TOP + NR, :], beside("depth", 1)),
            remote(stage, f, 1, source.at[f, pl.ds(d0, 4), rows, :],
                   target.at[f, 4 + ND : 8 + ND, TOP : TOP + NR, :], beside("depth", -1)),
            remote(stage, f, 2, source.at[f, layers, pl.ds(r0 + NR - 8, 8), :],
                   target.at[f, 4 : 4 + ND, 0:TOP, :], beside("row", 1)),
            remote(stage, f, 3, source.at[f, layers, pl.ds(r0, 8), :],
                   target.at[f, 4 : 4 + ND, TOP + NR : 2 * TOP + NR, :], beside("row", -1)),
        ]

    def column_copies(stage, f):
        return [
            remote(stage, f, 4, pack.at[stage, f], got.at[stage, 0, f], beside("col", 1)),
            remote(stage, f, 5, pack.at[stage, f], got.at[stage, 1, f], beside("col", -1)),
        ]

    def packed(carry, values, d):
        return jnp.where(lane_group == d, pltpu.roll(values, 4 + 8 * d, 1), carry)

    pl.semaphore_wait(barrier, len(peers))
    for f in FIELDS:
        for copy in face_copies(0, f):
            copy.start()
    for f in FIELDS:
        load_field(f).wait()

        def pack_layer(d, carry):
            return packed(carry, ext1[f, 4 + d, TOP : TOP + NR, :], d)

        pack[0, f] = lax.fori_loop(0, ND, pack_layer, jnp.zeros((NR, LANES), jnp.float32))
        for copy in column_copies(0, f):
            copy.start()

    def rates(ext):
        def one(d, carry):
            where = pl.ds(2 * d, 2)
            body = pl.ds(4 + 2 * d, 2)
            v0, v1, v3 = (ext[f, body, TOP : TOP + NR, :] for f in (0, 1, 3))
            rate[where] = 2.0 * v0 * v1 * jax.nn.sigmoid(8.0 * (v3 - 0.5))
            return carry

        lax.fori_loop(0, ND // 2, one, 0)

    chunk_lane = lax.broadcasted_iota(jnp.int32, (GROUP * NR, LANES), 1)

    def tendency(ext, f, start, border):
        def window(depth_shift, row_shift):
            block = ext[f, pl.ds(start + 4 + depth_shift, GROUP), TOP + row_shift : TOP + NR + row_shift, :]
            return block.reshape(GROUP * NR, LANES)

        centre = window(0, 0)
        edge = jnp.concatenate([pltpu.roll(border, 124 - 8 * (start + i), 1) for i in range(GROUP)], 0)
        laplace = 3.0 * CENTER_COEF * centre
        advect = None
        for spatial in range(3):
            gradient = None
            for offset in range(1, 5):
                if spatial == 0:
                    ahead, behind = window(offset, 0), window(-offset, 0)
                elif spatial == 1:
                    ahead, behind = window(0, offset), window(0, -offset)
                else:
                    ahead = pltpu.roll(jnp.where(chunk_lane < offset, edge, centre), LANES - offset, 1)
                    behind = pltpu.roll(jnp.where(chunk_lane >= LANES - offset, edge, centre), offset, 1)
                term = FIRST_COEF[offset - 1] * (ahead - behind)
                gradient = term if gradient is None else gradient + term
                laplace = laplace + SECOND_COEF[offset - 1] * (ahead + behind)
            flow = vel[spatial, pl.ds(start, GROUP)].reshape(GROUP * NR, LANES)
            advect = flow * gradient if advect is None else advect + flow * gradient
        source = SOURCE[f] * rate[pl.ds(start, GROUP)].reshape(GROUP * NR, LANES)
        return centre, DIFFUSIVITY[f] * laplace - advect + source

    def border_of(stage, f):
        return jnp.where(lane % 8 < 4, got[stage, 0, f], got[stage, 1, f])

    def arrived(stage, f):
        for copy in face_copies(stage, f) + column_copies(stage, f):
            copy.wait_recv()

    rates(ext1)
    load_velocity.wait()
    for f in FIELDS:
        arrived(0, f)
        border = border_of(0, f)

        def first_stage(c, carry):
            start = c * GROUP
            centre, tend = tendency(ext1, f, start, border)
            middle = (centre + 0.2 * tend).reshape(GROUP, NR, LANES)
            ext2[f, pl.ds(start + 4, GROUP), TOP : TOP + NR, :] = middle
            for i in range(GROUP):
                carry = packed(carry, middle[i], start + i)
            return carry

        pack[1, f] = lax.fori_loop(0, ND // GROUP, first_stage, jnp.zeros((NR, LANES), jnp.float32))
        for copy in face_copies(1, f) + column_copies(1, f):
            copy.start()

    rates(ext2)

    def store_field(f):
        return pltpu.make_async_copy(out.at[f], new_state.at[f], out_sem.at[f])

    def second(f):
        arrived(1, f)
        border = border_of(1, f)

        def second_stage(c, carry):
            start = c * GROUP
            centre, tend = tendency(ext2, f, start, border)
            before = ext1[f, pl.ds(start + 4, GROUP), TOP : TOP + NR, :].reshape(GROUP * NR, LANES)
            out[f, pl.ds(start, GROUP)] = (0.5 * (before + centre) + 0.1 * tend).reshape(GROUP, NR, LANES)
            return carry

        lax.fori_loop(0, ND // GROUP, second_stage, 0)
        store_field(f).start()

    second(3)

    from_column = lax.broadcasted_iota(jnp.int32, (LANES, LANES), 0).astype(jnp.float32)
    to_lane = lax.broadcasted_iota(jnp.int32, (LANES, LANES), 1)
    to_column = lax.rem(to_lane, PIX).astype(jnp.float32)
    spot = jnp.clip((to_column + 0.5) * 2.0 - 0.5, 0.0, LANES - 1.0)
    filter_all = jnp.maximum(0.0, 1.0 - jnp.abs(spot - from_column) / 2.0) / 2.0
    for half in range(2):
        part_filter = jnp.where(to_lane // PIX == half, filter_all, 0.0).astype(jnp.bfloat16)
        rest = out[3, half * 8 : half * 8 + 8].reshape(LANES, LANES)
        for piece in range(3):
            coarse = rest.astype(jnp.bfloat16)
            if piece < 2:
                rest = rest - coarse.astype(jnp.float32)
            term = jnp.dot(coarse, part_filter, preferred_element_type=jnp.float32)
            total = term if half == 0 and piece == 0 else total + term
    texture[...] = total

    words = table[0:1, :] + table[1:2, :] * 256 + table[2:3, :] * 65536 + (table[3:4, :] << 24)
    low, high = (jnp.broadcast_to(words[:, i * LANES : (i + 1) * LANES], (8, LANES)) for i in range(2))
    small_lane = lax.broadcasted_iota(jnp.int32, (8, LANES), 1)
    sub = lax.broadcasted_iota(jnp.int32, (8, LANES), 0)
    high_next = pltpu.roll(high, LANES - 1, 1)
    low_next = jnp.where(small_lane == LANES - 1, high_next, pltpu.roll(low, LANES - 1, 1))
    near_half = small_lane < PIX
    lowest_first = jnp.broadcast_to(order[0, 0], (8, LANES)) == 0
    first_half_front = lowest_first == near_half
    far_slice = 8 * (small_lane // PIX)

    def looked_up(sample):
        level = jnp.clip(sample, 0.0, 1.0) * 255.0
        lower = jnp.minimum(jnp.floor(level), 254.0)
        fraction = level - lower
        index = lower.astype(jnp.int32)
        place = index & (LANES - 1)
        upper_half = index >= LANES

        def pick(first, second_table):
            one = jnp.take_along_axis(first, place, axis=1, mode="promise_in_bounds")
            two = jnp.take_along_axis(second_table, place, axis=1, mode="promise_in_bounds")
            return jnp.where(upper_half, two, one)

        below, above = pick(low, high), pick(low_next, high_next)
        channels = []
        for c in range(4):
            b, a = ((lax.shift_right_logical(w, 8 * c) & 255).astype(jnp.float32) for w in (below, above))
            channels.append(b + (a - b) * fraction)
        return channels

    def part_copy(step):
        peer = lax.rem(my_depth + step, n_depth)
        return pltpu.make_async_remote_copy(
            src_ref=part.at[peer], dst_ref=mixed.at[my_depth], send_sem=part_send.at[step],
            recv_sem=part_recv.at[my_depth], device_id={"depth": peer}, device_id_type=MESH)

    def part_arrival(step):
        peer = lax.rem(my_depth + step, n_depth)
        return pltpu.make_async_remote_copy(
            src_ref=part.at[peer], dst_ref=mixed.at[peer], send_sem=part_send.at[step],
            recv_sem=part_recv.at[peer], device_id={"depth": peer}, device_id_type=MESH)

    def final_copy(step):
        peer = lax.rem(my_depth + step, n_depth)
        return pltpu.make_async_remote_copy(
            src_ref=final.at[my_depth], dst_ref=final.at[my_depth], send_sem=fin_send.at[step],
            recv_sem=fin_recv.at[my_depth], device_id={"depth": peer}, device_id_type=MESH)

    def final_arrival(step):
        peer = lax.rem(my_depth + step, n_depth)
        return pltpu.make_async_remote_copy(
            src_ref=final.at[peer], dst_ref=final.at[peer], send_sem=fin_send.at[step],
            recv_sem=fin_recv.at[peer], device_id={"depth": peer}, device_id_type=MESH)

    def rendered(block):
        base = jnp.clip(2 * block - 2 + (2 * my_depth + 5) // 8, 0, NR - 4)
        row = (8 * block + sub).astype(jnp.float32)
        samples = []
        for pair in range(8):
            slice_at = (16 * my_depth + pair + far_slice).astype(jnp.float32)
            spot = jnp.clip((row + 0.5) * 0.25 - 0.5 + 2.0 * ((slice_at + 0.5) / SLICES - 0.5), 0.0, NR - 1.0)
            sample = None
            for i in range(4):
                weight = jnp.maximum(0.0, 1.0 - jnp.abs(spot - (base + i).astype(jnp.float32)))
                term = weight * texture[pl.ds(pair * NR + base + i, 1), :]
                sample = term if sample is None else sample + term
            samples.append(sample)
        clear = jnp.ones((8, LANES), jnp.float32)
        sums = [jnp.zeros((8, LANES), jnp.float32) for _ in range(4)]
        for k in range(8):
            channels = looked_up(jnp.where(lowest_first, samples[k], samples[7 - k]))
            alpha = channels[3] * (6.0 / SLICES / 255.0)
            weight = clear * alpha
            scaled = weight * (1.0 / 255.0)
            for c in range(3):
                sums[c] = sums[c] + scaled * channels[c]
            sums[3] = sums[3] + weight
            clear = clear - weight
        turned = [pltpu.roll(value, PIX, 1) for value in sums]
        front_alpha = jnp.where(first_half_front, sums[3], turned[3])
        pieces = []
        for c in (0, 2):
            near = jnp.where(near_half, sums[c], turned[c + 1])
            far = jnp.where(near_half, turned[c], sums[c + 1])
            front = jnp.where(lowest_first, near, far)
            back = jnp.where(lowest_first, far, near)
            pieces.append(front + (1.0 - front_alpha) * back)
        return pieces

    for step in (4, 3, 5, 2, 6, 1, 7, 0):
        block = lax.rem(my_depth + step, n_depth)
        pieces = rendered(block)
        for i in range(2):
            if step:
                part[block, i] = pieces[i]
            else:
                mixed[my_depth, i] = pieces[i]
        if step:
            part_copy(step).start()

    for f in FIELDS[1:]:
        second(f)

    for step in range(1, n_depth):
        part_arrival(step).wait_recv()
    clear = jnp.ones((8, LANES), jnp.float32)
    sums = [jnp.zeros((8, LANES), jnp.float32) for _ in range(2)]
    for k in range(n_depth):
        pair = [jnp.where(lowest_first, mixed[k, i], mixed[n_depth - 1 - k, i]) for i in range(2)]
        alpha = jnp.where(near_half, pltpu.roll(pair[1], PIX, 1), pair[1])
        sums = [total + clear * value for total, value in zip(sums, pair)]
        clear = clear * (1.0 - alpha)
    for i in range(2):
        final[my_depth, i] = sums[i]
    for step in (4, 3, 5, 2, 6, 1, 7):
        final_copy(step).start()
    for stage in range(2):
        for f in FIELDS:
            for copy in face_copies(stage, f) + column_copies(stage, f):
                copy.wait_send()
    for step in range(1, n_depth):
        part_copy(step).wait_send()
    for f in FIELDS:
        store_field(f).wait()
    for step in range(1, n_depth):
        final_arrival(step).wait_recv()
    for block in range(n_depth):
        for i in range(2):
            value = final[block, i]
            image[2 * i, 8 * block : 8 * block + 8, :] = value[:, :PIX]
            image[2 * i + 1, 8 * block : 8 * block + 8, :] = value[:, PIX:]
    for step in range(1, n_depth):
        final_copy(step).wait_send()


def solution(mesh):
    sizes = tuple(mesh.shape[axis] for axis in ("depth", "row", "col"))
    f32 = jnp.float32
    any_space = pl.BlockSpec(memory_space=pl.ANY)
    vmem = pl.BlockSpec(memory_space=pltpu.VMEM)
    smem = pl.BlockSpec(memory_space=pltpu.SMEM)
    extended = (4, ND + 8, NR + 16, LANES)

    def local(state, velocity, view_order, tf_table):
        return tuple(pl.pallas_call(
            functools.partial(kernel, sizes),
            out_shape=(
                jax.ShapeDtypeStruct((4, ND, NR, LANES), f32),
                jax.ShapeDtypeStruct((4, PIX, PIX), f32),
            ),
            in_specs=[any_space, any_space, smem, vmem],
            out_specs=(any_space, vmem),
            scratch_shapes=[
                pltpu.VMEM(extended, f32),
                pltpu.VMEM(extended, f32),
                pltpu.VMEM((3, ND, NR, LANES), f32),
                pltpu.VMEM((ND, NR, LANES), f32),
                pltpu.VMEM((4, ND, NR, LANES), f32),
                pltpu.VMEM((2, 4, NR, LANES), f32),
                pltpu.VMEM((2, 2, 4, NR, LANES), f32),
                pltpu.VMEM((LANES, LANES), f32),
                pltpu.VMEM((8, 2, 8, LANES), f32),
                pltpu.VMEM((8, 2, 8, LANES), f32),
                pltpu.VMEM((8, 2, 8, LANES), f32),
                pltpu.SemaphoreType.DMA((4,)),
                pltpu.SemaphoreType.DMA,
                pltpu.SemaphoreType.DMA((4,)),
                pltpu.SemaphoreType.DMA((2, 4, 6)),
                pltpu.SemaphoreType.DMA((2, 4, 6)),
                pltpu.SemaphoreType.DMA((8,)),
                pltpu.SemaphoreType.DMA((8,)),
                pltpu.SemaphoreType.DMA((8,)),
                pltpu.SemaphoreType.DMA((8,)),
            ],
            compiler_params=pltpu.CompilerParams(collective_id=0, has_side_effects=True),
        )(state, velocity, view_order, tf_table))

    return jax.shard_map(
        local,
        mesh=mesh,
        in_specs=(P(None, "depth", "row", "col"), P(None, "depth", "row", "col"), P("row", "col"), P()),
        out_specs=(P(None, "depth", "row", "col"), P(None, "row", "col")),
        check_vma=False,
    )
```

time: 200 us -> 44.7 us (0.22)
  starting transfers between devices: 55.3 us -> 0 us
  matrix products: 46.3 us -> 0 us
  waiting for transfers between devices: 41.6 us -> 0 us
  Pallas kernels: 0 us -> 40.6 us
  loops' own time: 21.5 us -> 0 us
  local copies, waits for them, and re-layouts: 18.2 us -> 2.56 us
  other arithmetic: 13.3 us -> 0 us
    ppermute x15 -> x0, starting transfers between devices: 48.1 us -> none  [the longest x6 21.2 us: extended(): lax.ppermute(initial, axis, [(b, a) for a, b in up])]
    dot_general x18 -> x0, matrix products: 46.3 us -> none  [the longest x16 44.6 us: shade(): jnp.dot(table_values, weights, preferred_element_type=jnp.float32, precis...]
    pallas_call x0 -> x1, Pallas kernels: none -> 40.6 us  [local(): pl.pallas_call(functools.partial(kernel, sizes), out_shape=(jax.ShapeDtyp...]
    ppermute x15 -> x0, waiting for transfers between devices: 33.2 us -> none  [the longest x6 15.9 us: extended(): lax.ppermute(initial, axis, [(b, a) for a, b in up])]
    another operation x1 -> x0, loops' own time: 21.5 us -> none  [march_slices(): lax.scan(advance, start, jnp.arange(slice_count, dtype=jnp.int32))]
    dynamic_slice x16 -> x0, local copies, waits for them, and re-layouts: 9.38 us -> none  [march_slices(): lax.scan(advance, start, jnp.arange(slice_count, dtype=jnp.int32))]
    all_to_all x1 -> x0, waiting for transfers between devices: 8.36 us -> none  [copy_for_each(): return lax.all_to_all(copies, axis, split_axis=0, concat_axis=0, tiled=True)]
    add x20 -> x0, other arithmetic: 8.04 us -> none  [the longest x2 2.81 us: tendency(): laplace = laplace + SECOND_COEF[offset] * (forward + backward)]
  transfers between devices with their start and end apart: 16 -> 0, of which waited for: 8 -> 0; matrix products, arithmetic and copies ran while one was open for 3% -> 0% of each run, Pallas kernels for 0% -> 0%
where the time goes in v1:
time: 44.7 us; the launch traced here: 44.5 us
  Pallas kernels  40.6 us (91%)
  local copies, waits for them, and re-layouts  2.56 us (6%)
  between operations  1.29 us (3%)
    pallas_call x1, Pallas kernels, local(): pl.pallas_call(functools.partial(kernel, sizes), out_shape=(jax.ShapeDtyp...  40.6 us
    unnamed x4, local copies, waits for them, and re-layouts  2.56 us

profile of v1, /device:TPU:6, one launch (start us, length us, event | category | flops | bytes accessed | tf_op | source)
XLA Modules:
  0.0 44.5 jit_solution(7393131962467384635)
XLA Ops:
  1.3 40.6 %shard_map.59 = (f32[4,16,16,128]{3,2,1,0:T(8,128)}, f32[4,64,64]{2,1,0:T(8,128)}) custom-call(f32[4,16,16,128]{3,2,1,0:T(8,128)} %state.1, f32[3,16,16,128]{3,2,1,0:T(8,128)} %velocity.1, s32[1,1]{1,0:T(1,128)S(6)} %copy.8.order, s32[4,256]{1,0:T(4,128)} %table.1), custom_call_target="tpu_custom_call" | custom-call | tf_op jit(solution)/shard_map/pallas_call | solution.py:345
  41.9 0.0 copy-start
  41.9 1.9 %copy.9 = f32[4,16,16,128]{3,2,1,0:T(8,128)} copy(f32[4,16,16,128]{3,2,1,0:T(8,128)} %get-tuple-element.4) | data formatting | bytes 1048576
  43.8 0.0 copy-done
  43.8 0.7 %copy.10 = f32[4,64,64]{2,1,0:T(8,128)} copy(f32[4,64,64]{2,1,0:T(8,128)S(1)} %copy-done) | data formatting | bytes 131072
Async XLA Ops:
  41.9 1.9 %copy-start = (f32[4,64,64]{2,1,0:T(8,128)S(1)}, f32[4,64,64]{2,1,0:T(8,128)}, u32[]{:S(2)}) copy-start(f32[4,64,64]{2,1,0:T(8,128)} %get-tuple-element.5) | copy-start | bytes 196612

commit v2 on v1

v2 whole, which is shorter than its diff:
```python
import functools

import jax
import jax.numpy as jnp
from jax import lax
from jax.experimental import pallas as pl
from jax.experimental.pallas import tpu as pltpu
from jax.sharding import PartitionSpec as P

MESH = pl.DeviceIdType.MESH
FIRST_COEF = (0.8, -0.2, 4.0 / 105.0, -1.0 / 280.0)
SECOND_COEF = (1.6, -0.2, 8.0 / 315.0, -1.0 / 560.0)
CENTER_COEF = -205.0 / 72.0
DIFFUSIVITY = (0.05, 0.04, 0.03, 0.08)
SOURCE = (-1.0, -1.5, 2.5, 0.8)
FIELDS = (3, 0, 1, 2)
ND = 16
NR = 16
LANES = 128
TOP = 8
CHUNK = 4
ROWS = CHUNK * NR
SLICES = 128
PIX = 64


def kernel(sizes, state, velocity, order_in, table_in, new_state, image, ext1, ext2, vel, rate, partial, out, pack, got,
           flow_pack, weights, filters, words, order, table, texture, part, mixed, final, in_sem, vel_sem, small_sem, out_sem,
           send_sem, recv_sem, part_send, part_recv, fin_send, fin_recv, token):
    n_depth, n_row, n_col = sizes
    my_depth, my_row, my_col = lax.axis_index("depth"), lax.axis_index("row"), lax.axis_index("col")
    places = {"depth": (my_depth, n_depth), "row": (my_row, n_row), "col": (my_col, n_col)}

    def beside(axis, step):
        at, count = places[axis]
        return {axis: lax.rem(at + step + count, count)}

    barrier = pltpu.get_barrier_semaphore()
    neighbours = [beside(axis, step) for axis in ("depth", "row", "col") for step in (1, -1)]
    for peer in neighbours:
        pl.semaphore_signal(barrier, inc=1, device_id=peer, device_id_type=MESH)

    def load_field(f):
        return pltpu.make_async_copy(state.at[f], ext1.at[f, 4 : 4 + ND, TOP : TOP + NR, :], in_sem.at[f])

    load_velocity = pltpu.make_async_copy(velocity, vel, vel_sem)
    load_order = pltpu.make_async_copy(order_in, order, small_sem.at[0])
    load_table = pltpu.make_async_copy(table_in, table, small_sem.at[1])
    for f in FIELDS:
        load_field(f).start()
    load_velocity.start()
    load_order.start()
    load_table.start()

    lane = lax.broadcasted_iota(jnp.int32, (NR, LANES), 1)
    chunk_lane = lax.broadcasted_iota(jnp.int32, (ROWS, LANES), 1)
    chunk_edge = (chunk_lane < 4) | (chunk_lane >= LANES - 4)
    small_lane = lax.broadcasted_iota(jnp.int32, (8, LANES), 1)
    sub = lax.broadcasted_iota(jnp.int32, (8, LANES), 0)
    near_half = small_lane < PIX
    in_group = lane & 7
    low_side = in_group < 4

    def row_base(block):
        return jnp.clip(2 * block - 2 + (2 * my_depth + 5) // 8, 0, NR - 4)

    far_slice = 8 * (small_lane // PIX)
    for block in range(8):
        base = row_base(block)
        row = (8 * block + sub).astype(jnp.float32)
        slice_at = (16 * my_depth + far_slice).astype(jnp.float32)
        first_spot = (row + 0.5) * 0.25 - 0.5 + 2.0 * ((slice_at + 0.5) / SLICES - 0.5)
        for pair in range(8):
            spot = jnp.clip(first_spot + pair * (2.0 / SLICES), 0.0, NR - 1.0) - base.astype(jnp.float32)
            for i in range(4):
                weights[block, pair, i] = jnp.maximum(0.0, 1.0 - jnp.abs(spot - float(i)))
    from_column = lax.broadcasted_iota(jnp.int32, (LANES, LANES), 0).astype(jnp.float32)
    to_lane = lax.broadcasted_iota(jnp.int32, (LANES, LANES), 1)
    to_column = (to_lane & (PIX - 1)).astype(jnp.float32)
    spot = jnp.clip((to_column + 0.5) * 2.0 - 0.5, 0.0, LANES - 1.0)
    filter_all = jnp.maximum(0.0, 1.0 - jnp.abs(spot - from_column) / 2.0) / 2.0
    for half in range(2):
        filters[half] = jnp.where(to_lane // PIX == half, filter_all, 0.0).astype(jnp.bfloat16)

    def remote(stage, f, index, source, target, peer):
        return pltpu.make_async_remote_copy(
            src_ref=source, dst_ref=target, send_sem=send_sem.at[stage, f, index],
            recv_sem=recv_sem.at[stage, f, index], device_id=peer, device_id_type=MESH)

    def face_copies(stage, f):
        if stage == 0:
            source, target, d0, r0 = state, ext1, 0, 0
        else:
            source, target, d0, r0 = ext2, ext2, 4, TOP
        rows, layers = pl.ds(r0, NR), pl.ds(d0, ND)
        return [
            remote(stage, f, 0, source.at[f, pl.ds(d0 + ND - 4, 4), rows, :],
                   target.at[f, 0:4, TOP : TOP + NR, :], beside("depth", 1)),
            remote(stage, f, 1, source.at[f, pl.ds(d0, 4), rows, :],
                   target.at[f, 4 + ND : 8 + ND, TOP : TOP + NR, :], beside("depth", -1)),
            remote(stage, f, 2, source.at[f, layers, pl.ds(r0 + NR - 8, 8), :],
                   target.at[f, 4 : 4 + ND, 0:TOP, :], beside("row", 1)),
            remote(stage, f, 3, source.at[f, layers, pl.ds(r0, 8), :],
                   target.at[f, 4 : 4 + ND, TOP + NR : 2 * TOP + NR, :], beside("row", -1)),
        ]

    def column_copies(stage, f):
        return [
            remote(stage, f, 4, pack.at[stage, f], got.at[stage, 0, f], beside("col", 1)),
            remote(stage, f, 5, pack.at[stage, f], got.at[stage, 1, f], beside("col", -1)),
        ]

    lane_group = lane // 8

    def packed(layers):
        gathered = None
        for d, values in enumerate(layers):
            turned = pltpu.roll(values, (4 + 8 * d) % LANES, 1)
            gathered = turned if d == 0 else jnp.where(lane_group == d, turned, gathered)
        return gathered

    def body(ext, f, d):
        return ext[f, 4 + d, TOP : TOP + NR, :]

    pl.semaphore_wait(barrier, len(neighbours))
    for f in FIELDS:
        for copy in face_copies(0, f):
            copy.start()
    for f in FIELDS:
        load_field(f).wait()
        pack[0, f] = packed([body(ext1, f, d) for d in range(ND)])
        for copy in column_copies(0, f):
            copy.start()

    def rates(ext):
        for d in range(0, ND, CHUNK):
            v0, v1, v3 = (ext[f, 4 + d : 4 + d + CHUNK, TOP : TOP + NR, :] for f in (0, 1, 3))
            rate[d : d + CHUNK] = 2.0 * v0 * v1 * jax.nn.sigmoid(8.0 * (v3 - 0.5))

    def flow(spatial, d):
        return vel[spatial, d : d + CHUNK].reshape(ROWS, LANES)

    def columns_part(ext, f):
        for d in range(0, ND, CHUNK):
            centre = ext[f, 4 + d : 4 + d + CHUNK, TOP : TOP + NR, :].reshape(ROWS, LANES)
            total = (3.0 * CENTER_COEF * DIFFUSIVITY[f]) * centre
            gradient = None
            for offset in range(1, 5):
                ahead, behind = pltpu.roll(centre, LANES - offset, 1), pltpu.roll(centre, offset, 1)
                term = FIRST_COEF[offset - 1] * (ahead - behind)
                gradient = term if gradient is None else gradient + term
                total = total + (SECOND_COEF[offset - 1] * DIFFUSIVITY[f]) * (ahead + behind)
            partial[f, d : d + CHUNK] = (total - flow(2, d) * gradient).reshape(CHUNK, NR, LANES)

    def edge_terms(stage, f):
        change = jnp.where(low_side, got[stage, 0, f], got[stage, 1, f]) - pack[stage, f]
        second = first = None
        for offset in range(1, 5):
            ahead, behind = pltpu.roll(change, LANES - offset, 1), pltpu.roll(change, offset, 1)
            reach = (low_side & (in_group + offset >= 4)) | ((in_group >= 4) & (in_group - offset <= 3))
            moved = jnp.where(reach, jnp.where(low_side, ahead, behind), 0.0)
            one, two = FIRST_COEF[offset - 1] * moved, (SECOND_COEF[offset - 1] * DIFFUSIVITY[f]) * moved
            first = one if first is None else first + one
            second = two if second is None else second + two
        first = jnp.where(low_side, first, -first)
        return second - flow_pack[...] * first

    def tendency(ext, f, edges, d):
        def window(depth_shift, row_shift):
            d0, r0 = d + 4 + depth_shift, TOP + row_shift
            return ext[f, d0 : d0 + CHUNK, r0 : r0 + NR, :].reshape(ROWS, LANES)

        total = partial[f, d : d + CHUNK].reshape(ROWS, LANES)
        total = total + SOURCE[f] * rate[d : d + CHUNK].reshape(ROWS, LANES)
        along_depth = along_rows = None
        for offset in range(1, 5):
            up, down = window(offset, 0), window(-offset, 0)
            ahead, behind = window(0, offset), window(0, -offset)
            total = total + (SECOND_COEF[offset - 1] * DIFFUSIVITY[f]) * ((up + down) + (ahead + behind))
            one, two = FIRST_COEF[offset - 1] * (up - down), FIRST_COEF[offset - 1] * (ahead - behind)
            along_depth = one if along_depth is None else along_depth + one
            along_rows = two if along_rows is None else along_rows + two
        total = total - (flow(0, d) * along_depth + flow(1, d) * along_rows)
        edge = jnp.concatenate([pltpu.roll(edges, (124 - 8 * (d + i)) % LANES, 1) for i in range(CHUNK)], 0)
        return window(0, 0), total + jnp.where(chunk_edge, edge, 0.0)

    def arrived(stage, f):
        for copy in face_copies(stage, f) + column_copies(stage, f):
            copy.wait_recv()

    load_velocity.wait()
    flow_pack[...] = packed([vel[2, d] for d in range(ND)])
    columns_part(ext1, 3)
    rates(ext1)
    for f in FIELDS[1:]:
        columns_part(ext1, f)

    def first_stage(f):
        arrived(0, f)
        edges = edge_terms(0, f)
        for d in range(0, ND, CHUNK):
            centre, tend = tendency(ext1, f, edges, d)
            ext2[f, 4 + d : 4 + d + CHUNK, TOP : TOP + NR, :] = (centre + 0.2 * tend).reshape(CHUNK, NR, LANES)
        for copy in face_copies(1, f):
            copy.start()
        pack[1, f] = packed([body(ext2, f, d) for d in range(ND)])
        for copy in column_copies(1, f):
            copy.start()

    for f in FIELDS:
        first_stage(f)
    columns_part(ext2, 3)
    rates(ext2)

    load_order.wait()
    load_table.wait()
    word = table[0:1, :] + table[1:2, :] * 256 + table[2:3, :] * 65536 + (table[3:4, :] << 24)
    low, high = (jnp.broadcast_to(word[:, i * LANES : (i + 1) * LANES], (8, LANES)) for i in range(2))
    high_next = pltpu.roll(high, LANES - 1, 1)
    words[0] = low
    words[1] = high
    words[2] = jnp.where(small_lane == LANES - 1, high_next, pltpu.roll(low, LANES - 1, 1))
    words[3] = high_next
    lowest_first = jnp.broadcast_to(order[...], (8, LANES)) == 0
    first_half_front = lowest_first == near_half

    def store_field(f):
        return pltpu.make_async_copy(out.at[f], new_state.at[f], out_sem.at[f])

    def second_stage(f):
        edges = edge_terms(1, f)
        for d in range(0, ND, CHUNK):
            centre, tend = tendency(ext2, f, edges, d)
            before = ext1[f, 4 + d : 4 + d + CHUNK, TOP : TOP + NR, :].reshape(ROWS, LANES)
            out[f, d : d + CHUNK] = (0.5 * (before + centre) + 0.1 * tend).reshape(CHUNK, NR, LANES)
        store_field(f).start()

    arrived(1, 3)
    for side, peer in enumerate((beside("depth", 1), beside("depth", -1))):
        pl.semaphore_signal(token.at[side], inc=1, device_id=peer, device_id_type=MESH)
    second_stage(3)

    total = None
    for half in range(2):
        rest = out[3, half * 8 : half * 8 + 8].reshape(LANES, LANES)
        for piece in range(3):
            coarse = rest.astype(jnp.bfloat16)
            if piece < 2:
                rest = rest - coarse.astype(jnp.float32)
            term = jnp.dot(coarse, filters[half], preferred_element_type=jnp.float32)
            total = term if total is None else total + term
    texture[...] = total * 255.0

    def looked_up(sample):
        level = jnp.clip(sample, 0.0, 255.0)
        index = jnp.minimum(level.astype(jnp.int32), 254)
        fraction = level - index.astype(jnp.float32)
        place = index & (LANES - 1)
        upper_half = index >= LANES

        def pick(first):
            one = jnp.take_along_axis(words[first], place, axis=1, mode="promise_in_bounds")
            two = jnp.take_along_axis(words[first + 1], place, axis=1, mode="promise_in_bounds")
            return jnp.where(upper_half, two, one)

        def channels(value):
            spread = [value & 255, lax.shift_right_logical(value, 8) & 255, lax.shift_right_logical(value, 16) & 255,
                      lax.shift_right_logical(value, 24)]
            return [channel.astype(jnp.float32) for channel in spread]

        return channels(pick(0)), channels(pick(2)), fraction

    def peer_at(step):
        return lax.rem(my_depth + step, n_depth)

    def part_copy(step):
        peer = peer_at(step)
        return pltpu.make_async_remote_copy(
            src_ref=part.at[peer], dst_ref=mixed.at[my_depth], send_sem=part_send.at[step],
            recv_sem=part_recv.at[my_depth], device_id={"depth": peer}, device_id_type=MESH)

    def part_arrival(step):
        peer = peer_at(step)
        return pltpu.make_async_remote_copy(
            src_ref=part.at[peer], dst_ref=mixed.at[peer], send_sem=part_send.at[step],
            recv_sem=part_recv.at[peer], device_id={"depth": peer}, device_id_type=MESH)

    def final_copy(step):
        peer = peer_at(step)
        return pltpu.make_async_remote_copy(
            src_ref=final.at[my_depth], dst_ref=final.at[my_depth], send_sem=fin_send.at[step],
            recv_sem=fin_recv.at[my_depth], device_id={"depth": peer}, device_id_type=MESH)

    def final_arrival(step):
        peer = peer_at(step)
        return pltpu.make_async_remote_copy(
            src_ref=final.at[peer], dst_ref=final.at[peer], send_sem=fin_send.at[step],
            recv_sem=fin_recv.at[peer], device_id={"depth": peer}, device_id_type=MESH)

    def rendered(block):
        base = row_base(block)
        samples = []
        for pair in range(8):
            sample = None
            for i in range(4):
                term = weights[block, pair, i] * texture[pl.ds(pair * NR + base + i, 1), :]
                sample = term if sample is None else sample + term
            samples.append(sample)
        clear = jnp.ones((8, LANES), jnp.float32)
        sums = [jnp.zeros((8, LANES), jnp.float32) for _ in range(3)]
        for k in range(8):
            below, above, fraction = looked_up(jnp.where(lowest_first, samples[k], samples[7 - k]))
            alpha = (below[3] + (above[3] - below[3]) * fraction) * (6.0 / SLICES / 255.0)
            weight = clear * alpha
            share = weight * fraction
            keep = weight - share
            for c in range(3):
                sums[c] = sums[c] + (keep * below[c] + share * above[c])
            clear = clear - weight
        sums = [value * (1.0 / 255.0) for value in sums] + [1.0 - clear]
        turned = [pltpu.roll(value, PIX, 1) for value in sums]
        front_alpha = jnp.where(first_half_front, sums[3], turned[3])
        pieces = []
        for c in (0, 2):
            near = jnp.where(near_half, sums[c], turned[c + 1])
            far = jnp.where(near_half, turned[c], sums[c + 1])
            front = jnp.where(lowest_first, near, far)
            back = jnp.where(lowest_first, far, near)
            pieces.append(front + (1.0 - front_alpha) * back)
        return pieces

    for step in (4, 3, 5, 2, 6, 1, 7, 0):
        block = peer_at(step)
        pieces = rendered(block)
        for i in range(2):
            if step:
                part[block, i] = pieces[i]
            else:
                mixed[my_depth, i] = pieces[i]
        if step == 4:
            for side in range(2):
                pl.semaphore_wait(token.at[side], 1)
        if step:
            part_copy(step).start()

    for f in FIELDS[1:]:
        columns_part(ext2, f)
        arrived(1, f)
        second_stage(f)

    for step in range(1, n_depth):
        part_arrival(step).wait_recv()
    clear = jnp.ones((8, LANES), jnp.float32)
    sums = [jnp.zeros((8, LANES), jnp.float32) for _ in range(2)]
    for k in range(n_depth):
        pair = [jnp.where(lowest_first, mixed[k, i], mixed[n_depth - 1 - k, i]) for i in range(2)]
        alpha = jnp.where(near_half, pltpu.roll(pair[1], PIX, 1), pair[1])
        sums = [total + clear * value for total, value in zip(sums, pair)]
        clear = clear * (1.0 - alpha)
    for i in range(2):
        final[my_depth, i] = sums[i]
    for step in (4, 3, 5, 2, 6, 1, 7):
        final_copy(step).start()
    for stage in range(2):
        for f in FIELDS:
            for copy in face_copies(stage, f) + column_copies(stage, f):
                copy.wait_send()
    for step in range(1, n_depth):
        part_copy(step).wait_send()
    for f in FIELDS:
        store_field(f).wait()
    for step in range(1, n_depth):
        final_arrival(step).wait_recv()
    for block in range(n_depth):
        for i in range(2):
            value = final[block, i]
            image[2 * i, 8 * block : 8 * block + 8, :] = value[:, :PIX]
            image[2 * i + 1, 8 * block : 8 * block + 8, :] = value[:, PIX:]
    for step in range(1, n_depth):
        final_copy(step).wait_send()


def solution(mesh):
    sizes = tuple(mesh.shape[axis] for axis in ("depth", "row", "col"))
    f32 = jnp.float32
    any_space = pl.BlockSpec(memory_space=pl.ANY)
    vmem = pl.BlockSpec(memory_space=pltpu.VMEM)
    extended = (4, ND + 8, NR + 16, LANES)

    def local(state, velocity, view_order, tf_table):
        return tuple(pl.pallas_call(
            functools.partial(kernel, sizes),
            out_shape=(
                jax.ShapeDtypeStruct((4, ND, NR, LANES), f32),
                jax.ShapeDtypeStruct((4, PIX, PIX), f32),
            ),
            in_specs=[any_space] * 4,
            out_specs=(any_space, vmem),
            scratch_shapes=[
                pltpu.VMEM(extended, f32),
                pltpu.VMEM(extended, f32),
                pltpu.VMEM((3, ND, NR, LANES), f32),
                pltpu.VMEM((ND, NR, LANES), f32),
                pltpu.VMEM((4, ND, NR, LANES), f32),
                pltpu.VMEM((4, ND, NR, LANES), f32),
                pltpu.VMEM((2, 4, NR, LANES), f32),
                pltpu.VMEM((2, 2, 4, NR, LANES), f32),
                pltpu.VMEM((NR, LANES), f32),
                pltpu.VMEM((8, 8, 4, 8, LANES), f32),
                pltpu.VMEM((2, LANES, LANES), jnp.bfloat16),
                pltpu.VMEM((4, 8, LANES), jnp.int32),
                pltpu.VMEM((1, 1), jnp.int32),
                pltpu.VMEM((4, 2 * LANES), jnp.int32),
                pltpu.VMEM((LANES, LANES), f32),
                pltpu.VMEM((8, 2, 8, LANES), f32),
                pltpu.VMEM((8, 2, 8, LANES), f32),
                pltpu.VMEM((8, 2, 8, LANES), f32),
                pltpu.SemaphoreType.DMA((4,)),
                pltpu.SemaphoreType.DMA,
                pltpu.SemaphoreType.DMA((2,)),
                pltpu.SemaphoreType.DMA((4,)),
                pltpu.SemaphoreType.DMA((2, 4, 6)),
                pltpu.SemaphoreType.DMA((2, 4, 6)),
                pltpu.SemaphoreType.DMA((8,)),
                pltpu.SemaphoreType.DMA((8,)),
                pltpu.SemaphoreType.DMA((8,)),
                pltpu.SemaphoreType.DMA((8,)),
                pltpu.SemaphoreType.REGULAR((2,)),
            ],
            compiler_params=pltpu.CompilerParams(collective_id=0, has_side_effects=True),
        )(state, velocity, view_order, tf_table))

    return jax.shard_map(
        local,
        mesh=mesh,
        in_specs=(P(None, "depth", "row", "col"), P(None, "depth", "row", "col"), P("row", "col"), P()),
        out_specs=(P(None, "depth", "row", "col"), P(None, "row", "col")),
        check_vma=False,
    )
```

time: 44.7 us -> 37.5 us (0.84)
  Pallas kernels: 40.6 us -> 33.2 us
    pallas_call x1, Pallas kernels: 40.6 us -> 33.2 us  [local(): pl.pallas_call(functools.partial(kernel, sizes), out_shape=(jax.ShapeDtyp...]
where the time goes in v2:
time: 37.5 us; the launch traced here: 37 us
  Pallas kernels  33.2 us (89%)
  local copies, waits for them, and re-layouts  2.56 us (7%)
  between operations  1.29 us (3%)
    pallas_call x1, Pallas kernels, local(): pl.pallas_call(functools.partial(kernel, sizes), out_shape=(jax.ShapeDtyp...  33.2 us
    unnamed x4, local copies, waits for them, and re-layouts  2.56 us

profile of v2, /device:TPU:6, one launch (start us, length us, event | category | flops | bytes accessed | tf_op | source)
XLA Modules:
  0.0 37.0 jit_solution(16504183434911943006)
XLA Ops:
  1.3 33.2 %shard_map.59 = (f32[4,16,16,128]{3,2,1,0:T(8,128)}, f32[4,64,64]{2,1,0:T(8,128)}) custom-call(f32[4,16,16,128]{3,2,1,0:T(8,128)} %state.1, f32[3,16,16,128]{3,2,1,0:T(8,128)} %velocity.1, s32[1,1]{1,0:T(1,128)S(6)} %copy.8.order_in, s32[4,256]{1,0:T(4,128)} %table_in.1), custom_call_target="tpu_custom_call" | custom-call | tf_op jit(solution)/shard_map/pallas_call | solution.py:391
  34.4 0.0 copy-start
  34.5 1.9 %copy.9 = f32[4,16,16,128]{3,2,1,0:T(8,128)} copy(f32[4,16,16,128]{3,2,1,0:T(8,128)} %get-tuple-element.4) | data formatting | bytes 1048576
  36.4 0.0 copy-done
  36.4 0.7 %copy.10 = f32[4,64,64]{2,1,0:T(8,128)} copy(f32[4,64,64]{2,1,0:T(8,128)S(1)} %copy-done) | data formatting | bytes 131072
Async XLA Ops:
  34.4 1.9 %copy-start = (f32[4,64,64]{2,1,0:T(8,128)S(1)}, f32[4,64,64]{2,1,0:T(8,128)}, u32[]{:S(2)}) copy-start(f32[4,64,64]{2,1,0:T(8,128)} %get-tuple-element.5) | copy-start | bytes 196612

commit v3 on v2

--- a/solution.py
+++ b/solution.py
@@ -24,8 +24,8 @@
 PIX = 64
 
 
-def kernel(sizes, state, velocity, order_in, table_in, new_state, image, ext1, ext2, vel, rate, partial, out, pack, got,
-           flow_pack, weights, filters, words, order, table, texture, part, mixed, final, in_sem, vel_sem, small_sem, out_sem,
+def kernel(sizes, state, velocity, order_in, table_in, out, final, ext1, ext2, vel, rate, partial, pack, got,
+           flow_pack, weights, filters, words, order, table, texture, part, mixed, in_sem, vel_sem, small_sem,
            send_sem, recv_sem, part_send, part_recv, fin_send, fin_recv, token):
     n_depth, n_row, n_col = sizes
     my_depth, my_row, my_col = lax.axis_index("depth"), lax.axis_index("row"), lax.axis_index("col")
@@ -63,24 +63,6 @@
 
     def row_base(block):
         return jnp.clip(2 * block - 2 + (2 * my_depth + 5) // 8, 0, NR - 4)
-
-    far_slice = 8 * (small_lane // PIX)
-    for block in range(8):
-        base = row_base(block)
-        row = (8 * block + sub).astype(jnp.float32)
-        slice_at = (16 * my_depth + far_slice).astype(jnp.float32)
-        first_spot = (row + 0.5) * 0.25 - 0.5 + 2.0 * ((slice_at + 0.5) / SLICES - 0.5)
-        for pair in range(8):
-            spot = jnp.clip(first_spot + pair * (2.0 / SLICES), 0.0, NR - 1.0) - base.astype(jnp.float32)
-            for i in range(4):
-                weights[block, pair, i] = jnp.maximum(0.0, 1.0 - jnp.abs(spot - float(i)))
-    from_column = lax.broadcasted_iota(jnp.int32, (LANES, LANES), 0).astype(jnp.float32)
-    to_lane = lax.broadcasted_iota(jnp.int32, (LANES, LANES), 1)
-    to_column = (to_lane & (PIX - 1)).astype(jnp.float32)
-    spot = jnp.clip((to_column + 0.5) * 2.0 - 0.5, 0.0, LANES - 1.0)
-    filter_all = jnp.maximum(0.0, 1.0 - jnp.abs(spot - from_column) / 2.0) / 2.0
-    for half in range(2):
-        filters[half] = jnp.where(to_lane // PIX == half, filter_all, 0.0).astype(jnp.bfloat16)
 
     def remote(stage, f, index, source, target, peer):
         return pltpu.make_async_remote_copy(
@@ -98,10 +80,10 @@
                    target.at[f, 0:4, TOP : TOP + NR, :], beside("depth", 1)),
             remote(stage, f, 1, source.at[f, pl.ds(d0, 4), rows, :],
                    target.at[f, 4 + ND : 8 + ND, TOP : TOP + NR, :], beside("depth", -1)),
-            remote(stage, f, 2, source.at[f, layers, pl.ds(r0 + NR - 8, 8), :],
-                   target.at[f, 4 : 4 + ND, 0:TOP, :], beside("row", 1)),
-            remote(stage, f, 3, source.at[f, layers, pl.ds(r0, 8), :],
-                   target.at[f, 4 : 4 + ND, TOP + NR : 2 * TOP + NR, :], beside("row", -1)),
+            remote(stage, f, 2, source.at[f, layers, pl.ds(r0 + NR - 4, 4), :],
+                   target.at[f, 4 : 4 + ND, TOP - 4 : TOP, :], beside("row", 1)),
+            remote(stage, f, 3, source.at[f, layers, pl.ds(r0, 4), :],
+                   target.at[f, 4 : 4 + ND, TOP + NR : TOP + NR + 4, :], beside("row", -1)),
         ]
 
     def column_copies(stage, f):
@@ -123,19 +105,10 @@
         return ext[f, 4 + d, TOP : TOP + NR, :]
 
     pl.semaphore_wait(barrier, len(neighbours))
-    for f in FIELDS:
-        for copy in face_copies(0, f):
-            copy.start()
-    for f in FIELDS:
-        load_field(f).wait()
-        pack[0, f] = packed([body(ext1, f, d) for d in range(ND)])
-        for copy in column_copies(0, f):
-            copy.start()
-
-    def rates(ext):
+    def rates(ext, stage):
         for d in range(0, ND, CHUNK):
             v0, v1, v3 = (ext[f, 4 + d : 4 + d + CHUNK, TOP : TOP + NR, :] for f in (0, 1, 3))
-            rate[d : d + CHUNK] = 2.0 * v0 * v1 * jax.nn.sigmoid(8.0 * (v3 - 0.5))
+            rate[stage, d : d + CHUNK] = 2.0 * v0 * v1 * jax.nn.sigmoid(8.0 * (v3 - 0.5))
 
     def flow(spatial, d):
         return vel[spatial, d : d + CHUNK].reshape(ROWS, LANES)
@@ -165,13 +138,15 @@
         first = jnp.where(low_side, first, -first)
         return second - flow_pack[...] * first
 
-    def tendency(ext, f, edges, d):
+    def tendency(stage, f, edges, d):
+        ext = (ext1, ext2)[stage]
+
         def window(depth_shift, row_shift):
             d0, r0 = d + 4 + depth_shift, TOP + row_shift
             return ext[f, d0 : d0 + CHUNK, r0 : r0 + NR, :].reshape(ROWS, LANES)
 
         total = partial[f, d : d + CHUNK].reshape(ROWS, LANES)
-        total = total + SOURCE[f] * rate[d : d + CHUNK].reshape(ROWS, LANES)
+        total = total + SOURCE[f] * rate[stage, d : d + CHUNK].reshape(ROWS, LANES)
         along_depth = along_rows = None
         for offset in range(1, 5):
             up, down = window(offset, 0), window(-offset, 0)
@@ -184,33 +159,76 @@
         edge = jnp.concatenate([pltpu.roll(edges, (124 - 8 * (d + i)) % LANES, 1) for i in range(CHUNK)], 0)
         return window(0, 0), total + jnp.where(chunk_edge, edge, 0.0)
 
-    def arrived(stage, f):
-        for copy in face_copies(stage, f) + column_copies(stage, f):
-            copy.wait_recv()
-
+    def arrived(stage, f, indices):
+        copies = face_copies(stage, f) + column_copies(stage, f)
+        for index in indices:
+            copies[index].wait_recv()
+
+    def prepare():
+        far_slice = 8 * (small_lane // PIX)
+        for block in range(8):
+            base = row_base(block)
+            row = (8 * block + sub).astype(jnp.float32)
+            slice_at = (16 * my_depth + far_slice).astype(jnp.float32)
+            first_spot = (row + 0.5) * 0.25 - 0.5 + 2.0 * ((slice_at + 0.5) / SLICES - 0.5)
+            for pair in range(8):
+                spot = jnp.clip(first_spot + pair * (2.0 / SLICES), 0.0, NR - 1.0) - base.astype(jnp.float32)
+                for i in range(4):
+                    weights[block, pair, i] = jnp.maximum(0.0, 1.0 - jnp.abs(spot - float(i)))
+        from_column = lax.broadcasted_iota(jnp.int32, (LANES, LANES), 0).astype(jnp.float32)
+        to_lane = lax.broadcasted_iota(jnp.int32, (LANES, LANES), 1)
+        to_column = (to_lane & (PIX - 1)).astype(jnp.float32)
+        spot = jnp.clip((to_column + 0.5) * 2.0 - 0.5, 0.0, LANES - 1.0)
+        filter_all = jnp.maximum(0.0, 1.0 - jnp.abs(spot - from_column) / 2.0) / 2.0
+        for half in range(2):
+            filters[half] = jnp.where(to_lane // PIX == half, filter_all, 0.0).astype(jnp.bfloat16)
+
+    def send_first(f):
+        for copy in face_copies(0, f):
+            copy.start()
+        load_field(f).wait()
+        pack[0, f] = packed([body(ext1, f, d) for d in range(ND)])
+        for copy in column_copies(0, f):
+            copy.start()
+
+    send_first(3)
     load_velocity.wait()
     flow_pack[...] = packed([vel[2, d] for d in range(ND)])
     columns_part(ext1, 3)
-    rates(ext1)
-    for f in FIELDS[1:]:
-        columns_part(ext1, f)
+    send_first(0)
+    columns_part(ext1, 0)
+    send_first(1)
+    rates(ext1, 0)
+    columns_part(ext1, 1)
+    prepare()
 
     def first_stage(f):
-        arrived(0, f)
+        arrived(0, f, (2, 3, 4, 5))
         edges = edge_terms(0, f)
-        for d in range(0, ND, CHUNK):
-            centre, tend = tendency(ext1, f, edges, d)
+
+        def layers(d):
+            centre, tend = tendency(0, f, edges, d)
             ext2[f, 4 + d : 4 + d + CHUNK, TOP : TOP + NR, :] = (centre + 0.2 * tend).reshape(CHUNK, NR, LANES)
-        for copy in face_copies(1, f):
-            copy.start()
+
+        copies = face_copies(1, f)
+        for d in range(CHUNK, ND - CHUNK, CHUNK):
+            layers(d)
+        arrived(0, f, (0, 1))
+        layers(0)
+        copies[1].start()
+        layers(ND - CHUNK)
+        for index in (0, 2, 3):
+            copies[index].start()
         pack[1, f] = packed([body(ext2, f, d) for d in range(ND)])
         for copy in column_copies(1, f):
             copy.start()
 
-    for f in FIELDS:
-        first_stage(f)
+    first_stage(3)
+    send_first(2)
+    first_stage(0)
+    first_stage(1)
     columns_part(ext2, 3)
-    rates(ext2)
+    rates(ext2, 1)
 
     load_order.wait()
     load_table.wait()
@@ -224,21 +242,25 @@
     lowest_first = jnp.broadcast_to(order[...], (8, LANES)) == 0
     first_half_front = lowest_first == near_half
 
-    def store_field(f):
-        return pltpu.make_async_copy(out.at[f], new_state.at[f], out_sem.at[f])
-
-    def second_stage(f):
+    def second_stage(f, told=False):
+        arrived(1, f, (2, 3, 4, 5))
         edges = edge_terms(1, f)
-        for d in range(0, ND, CHUNK):
-            centre, tend = tendency(ext2, f, edges, d)
+
+        def layers(d):
+            centre, tend = tendency(1, f, edges, d)
             before = ext1[f, 4 + d : 4 + d + CHUNK, TOP : TOP + NR, :].reshape(ROWS, LANES)
             out[f, d : d + CHUNK] = (0.5 * (before + centre) + 0.1 * tend).reshape(CHUNK, NR, LANES)
-        store_field(f).start()
-
-    arrived(1, 3)
-    for side, peer in enumerate((beside("depth", 1), beside("depth", -1))):
-        pl.semaphore_signal(token.at[side], inc=1, device_id=peer, device_id_type=MESH)
-    second_stage(3)
+
+        for d in range(CHUNK, ND - CHUNK, CHUNK):
+            layers(d)
+        arrived(1, f, (0, 1))
+        if told:
+            for side, peer in enumerate((beside("depth", 1), beside("depth", -1))):
+                pl.semaphore_signal(token.at[side], inc=1, device_id=peer, device_id_type=MESH)
+        for d in (0, ND - CHUNK):
+            layers(d)
+
+    second_stage(3, True)
 
     total = None
     for half in range(2):
@@ -343,9 +365,10 @@
         if step:
             part_copy(step).start()
 
-    for f in FIELDS[1:]:
+    columns_part(ext1, 2)
+    first_stage(2)
+    for f in FIELDS[1:3]:
         columns_part(ext2, f)
-        arrived(1, f)
         second_stage(f)
 
     for step in range(1, n_depth):
@@ -361,23 +384,33 @@
         final[my_depth, i] = sums[i]
     for step in (4, 3, 5, 2, 6, 1, 7):
         final_copy(step).start()
+    columns_part(ext2, 2)
+    second_stage(2)
     for stage in range(2):
         for f in FIELDS:
             for copy in face_copies(stage, f) + column_copies(stage, f):
                 copy.wait_send()
     for step in range(1, n_depth):
         part_copy(step).wait_send()
-    for f in FIELDS:
-        store_field(f).wait()
     for step in range(1, n_depth):
         final_arrival(step).wait_recv()
-    for block in range(n_depth):
+    for step in range(1, n_depth):
+        final_copy(step).wait_send()
+
+
+def finish(out, final, new_state, image, tile, sem, tile_sem):
+    copies = [pltpu.make_async_copy(out.at[f], new_state.at[f], sem.at[f]) for f in range(4)]
+    for copy in copies:
+        copy.start()
+    for block in range(8):
         for i in range(2):
             value = final[block, i]
-            image[2 * i, 8 * block : 8 * block + 8, :] = value[:, :PIX]
-            image[2 * i + 1, 8 * block : 8 * block + 8, :] = value[:, PIX:]
-    for step in range(1, n_depth):
-        final_copy(step).wait_send()
+            tile[2 * i, 8 * block : 8 * block + 8, :] = value[:, :PIX]
+            tile[2 * i + 1, 8 * block : 8 * block + 8, :] = value[:, PIX:]
+    copies.append(pltpu.make_async_copy(tile, image, tile_sem))
+    copies[4].start()
+    for copy in copies:
+        copy.wait()
 
 
 def solution(mesh):
@@ -388,20 +421,16 @@
     extended = (4, ND + 8, NR + 16, LANES)
 
     def local(state, velocity, view_order, tf_table):
-        return tuple(pl.pallas_call(
+        held = pl.pallas_call(
             functools.partial(kernel, sizes),
-            out_shape=(
-                jax.ShapeDtypeStruct((4, ND, NR, LANES), f32),
-                jax.ShapeDtypeStruct((4, PIX, PIX), f32),
-            ),
+            out_shape=(pltpu.VMEM((4, ND, NR, LANES), f32), pltpu.VMEM((8, 2, 8, LANES), f32)),
             in_specs=[any_space] * 4,
-            out_specs=(any_space, vmem),
+            out_specs=(vmem, vmem),
             scratch_shapes=[
                 pltpu.VMEM(extended, f32),
                 pltpu.VMEM(extended, f32),
                 pltpu.VMEM((3, ND, NR, LANES), f32),
-                pltpu.VMEM((ND, NR, LANES), f32),
-                pltpu.VMEM((4, ND, NR, LANES), f32),
+                pltpu.VMEM((2, ND, NR, LANES), f32),
                 pltpu.VMEM((4, ND, NR, LANES), f32),
                 pltpu.VMEM((2, 4, NR, LANES), f32),
                 pltpu.VMEM((2, 2, 4, NR, LANES), f32),
@@ -414,11 +443,9 @@
                 pltpu.VMEM((LANES, LANES), f32),
                 pltpu.VMEM((8, 2, 8, LANES), f32),
                 pltpu.VMEM((8, 2, 8, LANES), f32),
-                pltpu.VMEM((8, 2, 8, LANES), f32),
                 pltpu.SemaphoreType.DMA((4,)),
                 pltpu.SemaphoreType.DMA,
                 pltpu.SemaphoreType.DMA((2,)),
-                pltpu.SemaphoreType.DMA((4,)),
                 pltpu.SemaphoreType.DMA((2, 4, 6)),
                 pltpu.SemaphoreType.DMA((2, 4, 6)),
                 pltpu.SemaphoreType.DMA((8,)),
@@ -428,7 +455,17 @@
                 pltpu.SemaphoreType.REGULAR((2,)),
             ],
             compiler_params=pltpu.CompilerParams(collective_id=0, has_side_effects=True),
-        )(state, velocity, view_order, tf_table))
+        )(state, velocity, view_order, tf_table)
+        return tuple(pl.pallas_call(
+            finish,
+            out_shape=(
+                jax.ShapeDtypeStruct((4, ND, NR, LANES), f32),
+                jax.ShapeDtypeStruct((4, PIX, PIX), f32),
+            ),
+            in_specs=[vmem, vmem],
+            out_specs=(any_space, any_space),
+            scratch_shapes=[pltpu.VMEM((4, PIX, PIX), f32), pltpu.SemaphoreType.DMA((4,)), pltpu.SemaphoreType.DMA],
+        )(*(pltpu.with_memory_space_constraint(value, pltpu.VMEM) for value in held)))
 
     return jax.shard_map(
         local,

time: 37.5 us -> 34.6 us (0.923)
  local copies, waits for them, and re-layouts: 2.56 us -> 0 us
    unnamed x4 -> x0, local copies, waits for them, and re-layouts: 2.56 us -> none
    pallas_call x1 -> x2, Pallas kernels: 33.2 us -> 32.9 us  [the longest x1 32.1 us: local(): pl.pallas_call(functools.partial(kernel, sizes), out_shape=(pltpu.VMEM((4...]
where the time goes in v3:
time: 34.6 us; the launch traced here: 34.2 us
  Pallas kernels  32.9 us (95%)
  between operations  1.28 us (4%)
    pallas_call x1, Pallas kernels, local(): pl.pallas_call(functools.partial(kernel, sizes), out_shape=(pltpu.VMEM((4...  32.1 us
    pallas_call x1, Pallas kernels, local(): pl.pallas_call(finish, out_shape=(jax.ShapeDtypeStruct((4, ND, NR, LANES)...  0.87 us

profile of v3, /device:TPU:6, one launch (start us, length us, event | category | flops | bytes accessed | tf_op | source)
XLA Modules:
  0.0 34.2 jit_solution(16992815956432651048)
XLA Ops:
  1.3 32.1 %shard_map.59 = (f32[4,16,16,128]{3,2,1,0:T(8,128)S(1)}, f32[8,2,8,128]{3,2,1,0:T(8,128)S(1)}) custom-call(f32[4,16,16,128]{3,2,1,0:T(8,128)} %state.1, f32[3,16,16,128]{3,2,1,0:T(8,128)} %velocity.1, s32[1,1]{1,0:T(1,128)S(6)} %copy.6.order_in, s32[4,256]{1,0:T(4,128)} %table_in.1), custom_call_target="tpu_custom_call" | custom-call | tf_op jit(solution)/shard_map/pallas_call | solution.py:424
  33.4 0.9 %shard_map.60 = (f32[4,16,16,128]{3,2,1,0:T(8,128)}, f32[4,64,64]{2,1,0:T(8,128)}) custom-call(f32[4,16,16,128]{3,2,1,0:T(8,128)S(1)} %get-tuple-element.4.out, f32[8,2,8,128]{3,2,1,0:T(8,128)S(1)} %get-tuple-element.5.final), custom_call_target="tpu_custom_call" | custom-call | tf_op jit(solution)/shard_map/pallas_call | solution.py:459

commit v4 on v3

--- a/solution.py
+++ b/solution.py
@@ -186,7 +186,8 @@
     def send_first(f):
         for copy in face_copies(0, f):
             copy.start()
-        load_field(f).wait()
+        if f > 1:
+            load_field(f).wait()
         pack[0, f] = packed([body(ext1, f, d) for d in range(ND)])
         for copy in column_copies(0, f):
             copy.start()
@@ -195,8 +196,10 @@
     load_velocity.wait()
     flow_pack[...] = packed([vel[2, d] for d in range(ND)])
     columns_part(ext1, 3)
+    load_field(0).wait()
     send_first(0)
     columns_part(ext1, 0)
+    load_field(1).wait()
     send_first(1)
     rates(ext1, 0)
     columns_part(ext1, 1)
@@ -224,9 +227,9 @@
             copy.start()
 
     first_stage(3)
-    send_first(2)
     first_stage(0)
     first_stage(1)
+    send_first(2)
     columns_part(ext2, 3)
     rates(ext2, 1)
 
@@ -351,19 +354,21 @@
             pieces.append(front + (1.0 - front_alpha) * back)
         return pieces
 
-    for step in (4, 3, 5, 2, 6, 1, 7, 0):
-        block = peer_at(step)
-        pieces = rendered(block)
-        for i in range(2):
-            if step:
-                part[block, i] = pieces[i]
-            else:
-                mixed[my_depth, i] = pieces[i]
-        if step == 4:
+    for steps in ((4,), (3, 5), (2, 6), (1, 7, 0)):
+        for step in steps:
+            block = peer_at(step)
+            pieces = rendered(block)
+            for i in range(2):
+                if step:
+                    part[block, i] = pieces[i]
+                else:
+                    mixed[my_depth, i] = pieces[i]
+        if steps[0] == 4:
             for side in range(2):
                 pl.semaphore_wait(token.at[side], 1)
-        if step:
-            part_copy(step).start()
+        for step in steps:
+            if step:
+                part_copy(step).start()
 
     columns_part(ext1, 2)
     first_stage(2)
@@ -417,6 +422,7 @@
     sizes = tuple(mesh.shape[axis] for axis in ("depth", "row", "col"))
     f32 = jnp.float32
     any_space = pl.BlockSpec(memory_space=pl.ANY)
+    hbm = pl.BlockSpec(memory_space=pltpu.HBM)
     vmem = pl.BlockSpec(memory_space=pltpu.VMEM)
     extended = (4, ND + 8, NR + 16, LANES)
 
@@ -424,7 +430,7 @@
         held = pl.pallas_call(
             functools.partial(kernel, sizes),
             out_shape=(pltpu.VMEM((4, ND, NR, LANES), f32), pltpu.VMEM((8, 2, 8, LANES), f32)),
-            in_specs=[any_space] * 4,
+            in_specs=[any_space, any_space, hbm, hbm],
             out_specs=(vmem, vmem),
             scratch_shapes=[
                 pltpu.VMEM(extended, f32),

time: 34.6 us -> 34.3 us (level)
  no operation moved by 1% of the time
where the time goes in v4:
time: 34.3 us; the launch traced here: 34.2 us
  Pallas kernels  32.9 us (96%)
  between operations  1.28 us (4%)
    pallas_call x1, Pallas kernels, local(): pl.pallas_call(functools.partial(kernel, sizes), out_shape=(pltpu.VMEM((4...  32 us
    pallas_call x1, Pallas kernels, local(): pl.pallas_call(finish, out_shape=(jax.ShapeDtypeStruct((4, ND, NR, LANES)...  0.87 us

profile of v4, /device:TPU:6, one launch (start us, length us, event | category | flops | bytes accessed | tf_op | source)
XLA Modules:
  0.0 34.2 jit_solution(619623263221241309)
XLA Ops:
  1.3 32.0 %shard_map.59 = (f32[4,16,16,128]{3,2,1,0:T(8,128)S(1)}, f32[8,2,8,128]{3,2,1,0:T(8,128)S(1)}) custom-call(f32[4,16,16,128]{3,2,1,0:T(8,128)} %state.1, f32[3,16,16,128]{3,2,1,0:T(8,128)} %velocity.1, s32[1,1]{1,0:T(1,128)S(6)} %copy.6.order_in, s32[4,256]{1,0:T(4,128)} %table_in.1), custom_call_target="tpu_custom_call" | custom-call | tf_op jit(solution)/shard_map/pallas_call | solution.py:430
  33.3 0.9 %shard_map.60 = (f32[4,16,16,128]{3,2,1,0:T(8,128)}, f32[4,64,64]{2,1,0:T(8,128)}) custom-call(f32[4,16,16,128]{3,2,1,0:T(8,128)S(1)} %get-tuple-element.4.out, f32[8,2,8,128]{3,2,1,0:T(8,128)S(1)} %get-tuple-element.5.final), custom_call_target="tpu_custom_call" | custom-call | tf_op jit(solution)/shard_map/pallas_call | solution.py:465

commit v5 on v4

--- a/solution.py
+++ b/solution.py
@@ -372,9 +372,6 @@
 
     columns_part(ext1, 2)
     first_stage(2)
-    for f in FIELDS[1:3]:
-        columns_part(ext2, f)
-        second_stage(f)
 
     for step in range(1, n_depth):
         part_arrival(step).wait_recv()
@@ -389,6 +386,9 @@
         final[my_depth, i] = sums[i]
     for step in (4, 3, 5, 2, 6, 1, 7):
         final_copy(step).start()
+    for f in FIELDS[1:3]:
+        columns_part(ext2, f)
+        second_stage(f)
     columns_part(ext2, 2)
     second_stage(2)
     for stage in range(2):

time: 34.3 us -> 34.3 us (level)
  no operation moved by 1% of the time
where the time goes in v5:
time: 34.3 us; the launch traced here: 34.2 us
  Pallas kernels  32.9 us (96%)
  between operations  1.28 us (4%)
    pallas_call x1, Pallas kernels, local(): pl.pallas_call(functools.partial(kernel, sizes), out_shape=(pltpu.VMEM((4...  32 us
    pallas_call x1, Pallas kernels, local(): pl.pallas_call(finish, out_shape=(jax.ShapeDtypeStruct((4, ND, NR, LANES)...  0.87 us

profile of v5, /device:TPU:6, one launch (start us, length us, event | category | flops | bytes accessed | tf_op | source)
XLA Modules:
  0.0 34.2 jit_solution(12621083683660142553)
XLA Ops:
  1.3 32.0 %shard_map.59 = (f32[4,16,16,128]{3,2,1,0:T(8,128)S(1)}, f32[8,2,8,128]{3,2,1,0:T(8,128)S(1)}) custom-call(f32[4,16,16,128]{3,2,1,0:T(8,128)} %state.1, f32[3,16,16,128]{3,2,1,0:T(8,128)} %velocity.1, s32[1,1]{1,0:T(1,128)S(6)} %copy.6.order_in, s32[4,256]{1,0:T(4,128)} %table_in.1), custom_call_target="tpu_custom_call" | custom-call | tf_op jit(solution)/shard_map/pallas_call | solution.py:430
  33.3 0.9 %shard_map.60 = (f32[4,16,16,128]{3,2,1,0:T(8,128)}, f32[4,64,64]{2,1,0:T(8,128)}) custom-call(f32[4,16,16,128]{3,2,1,0:T(8,128)S(1)} %get-tuple-element.4.out, f32[8,2,8,128]{3,2,1,0:T(8,128)S(1)} %get-tuple-element.5.final), custom_call_target="tpu_custom_call" | custom-call | tf_op jit(solution)/shard_map/pallas_call | solution.py:465
